TPU v7x, 128 devices: a whole 4x4x4 slice. The times are simulated.
128 devices in a mesh: grid: 32 (over z, x, core), rep: 4 (over y).
Axes of the slice: x: 4, y: 4, z: 4, core: 2. Of those that a mesh axis runs over, the one named last changes fastest.
Arguments:
- functions: bfloat16 [8192, 32768], P(('grid', 'rep')), may hold values from -6 to 6
- filter_taps: bfloat16 [16], replicated, may hold values from -0.59765625 to 0.59765625
- potential: float32 [32768], replicated, may hold values from 0 to 1
- energies: float32 [8192], P(('grid', 'rep')), may hold values from -1.5 to -0.5
- region_start: int32 [8192], P(('grid', 'rep')), may hold values from 0 to 128
- region_length: int32 [8192], P(('grid', 'rep')), may hold values from 256 to 384
- partner_groups: int32 [128, 3], replicated, may hold values from 0 to 127, as said below
Outputs:
- corrected: bfloat16 [8192, 32768], P(('grid', 'rep'))
Inputs may be any that keep to these rules, and one draw needn't show every extreme that they name: `partner_groups`: the 3 entries of a row are distinct and differ from the row's own group; each is the row's group plus an offset of magnitude 1 to 63, modulo 128.
All inputs are finite; a program needn't handle non-finite values.
Results may differ from a plain program's by a relative error of at most 0.005.
Values may be sent and summed in bfloat16 or wider, within the bound.
A program may use at most 128 MiB of HBM per device.

v0:
```python
import jax
import jax.numpy as jnp
from jax import lax
from jax.sharding import PartitionSpec as P

SIDE = 32
NC = 32768
BLOCK = 64
GROUP = 64
TAPS = 16
PARTNERS = 3
LMAX = 384


def filter_matrix(filter_taps, extent):
    centre = TAPS // 2
    inputs = jnp.arange(extent, dtype=jnp.int32)
    distance = inputs[:, None] - inputs[None, :] + centre
    choose = (distance[:, :, None] == jnp.arange(TAPS, dtype=jnp.int32)[None, None, :]).astype(
        jnp.float32
    )
    return jnp.sum(choose * filter_taps.astype(jnp.float32)[None, None, :], axis=2)


def on_device(
    functions, filter_taps, potential, energies, region_start, region_length, partner_groups
):
    count_rows = functions.shape[0]
    grid_size = lax.axis_size("grid")
    rep_size = lax.axis_size("rep")
    devices_all = grid_size * rep_size
    local_cols = NC // devices_all
    single = filter_matrix(filter_taps, SIDE)
    ident = jnp.eye(SIDE, dtype=jnp.float32)
    plane_matrix = (jnp.kron(single, ident) + jnp.kron(ident, single)).astype(jnp.bfloat16)
    line_matrix = single.astype(jnp.bfloat16)
    slabs = functions.reshape(count_rows, SIDE, SIDE * SIDE)
    plane_part = jnp.dot(
        functions.reshape(count_rows * SIDE, SIDE * SIDE),
        plane_matrix,
        preferred_element_type=jnp.float32,
    ).reshape(count_rows, SIDE, SIDE * SIDE)
    line_part = jnp.einsum("fxc,xw->fwc", slabs, line_matrix, preferred_element_type=jnp.float32)
    kinetic = (plane_part + line_part).reshape(count_rows, NC)
    values = functions.astype(jnp.float32)
    gradient = kinetic + potential[None, :] * values - energies[:, None] * values
    updated = values - 0.3 * gradient / (1.0 - energies)[:, None]
    block_index = jnp.arange(NC, dtype=jnp.int32) // BLOCK
    inside = (block_index[None, :] >= region_start[:, None]) & (
        block_index[None, :] < (region_start + region_length)[:, None]
    )
    refined = jnp.where(inside, updated, 0.0).astype(jnp.bfloat16)
    gridded = lax.all_to_all(refined, ("grid", "rep"), split_axis=1, concat_axis=0, tiled=True)
    group_count = gridded.shape[0] // GROUP
    grouped = gridded.reshape(group_count, GROUP, local_cols)
    partner_rows = grouped[partner_groups]
    stacked = jnp.concatenate([grouped[:, None], partner_rows], axis=1)
    local_intersection = jnp.einsum(
        "agc,akhc->akgh", grouped, stacked, preferred_element_type=jnp.float32
    )
    weight = 1.0 / (BLOCK * LMAX)
    identity_block = jnp.concatenate(
        [jnp.eye(GROUP, dtype=jnp.float32)[None], jnp.zeros((PARTNERS, GROUP, GROUP), jnp.float32)],
        axis=0,
    )
    summed = lax.psum(local_intersection, ("grid", "rep"))
    coupling = (0.5 * (summed * weight - identity_block[None])).astype(jnp.bfloat16)
    shifted = jnp.einsum("akgh,akhc->agc", coupling, stacked, preferred_element_type=jnp.float32)
    result_grid = (grouped.astype(jnp.float32) - shifted).astype(jnp.bfloat16)
    result_grid = result_grid.reshape(group_count * GROUP, local_cols)
    return lax.all_to_all(result_grid, ("grid", "rep"), split_axis=0, concat_axis=1, tiled=True)


def solution(mesh):
    return jax.shard_map(
        on_device,
        mesh=mesh,
        in_specs=(
            P(("grid", "rep"), None),
            P(),
            P(),
            P(("grid", "rep")),
            P(("grid", "rep")),
            P(("grid", "rep")),
            P(),
        ),
        out_specs=P(("grid", "rep"), None),
        check_vma=False,
    )
```

profile of v0, /device:TPU:1, one launch (start us, length us, event | category | flops | bytes accessed | tf_op | source)
XLA Modules:
  0.0 433.6 jit_solution(11363357073585440919)
XLA Ops:
  6.6 0.7 convert_element_type.56
  7.2 0.1 select_reduce_fusion
  7.4 5.9 %add_convert_fusion = bf16[32,32,32,32]{3,2,1,0:T(8,128)(2,1)} fusion(f32[32,32]{1,0:T(8,128)S(1)} %select_reduce_fusion, f32[32,32]{1,0:T(8,128)S(1)} %fusion.13), kind=kLoop, calls=%fused_computation.2 | loop fusion | flops 4194304 | bytes 2105344 | tf_op jit(solution)/shard_map/convert_element_type | solution.py:35
  13.3 11.3 %convert_element_type.59 = bf16[1024,1024]{1,0:T(8,128)(2,1)S(1)} reshape(bf16[32,32,32,32]{3,2,1,0:T(8,128)(2,1)} %add_convert_fusion) | data formatting | bytes 4194304 | tf_op jit(solution)/shard_map/convert_element_type | solution.py:35
  24.6 7.4 %reshape.111 = bf16[2048,1024]{1,0:T(8,128)(2,1)} reshape(bf16[64,32768]{1,0:T(8,128)(2,1)} %param.7) | data formatting | bytes 8388608 | tf_op jit(solution)/shard_map/reshape | solution.py:39
  32.0 9.0 %convolution_bitcast_fusion = f32[2048,1024]{0,1:T(8,128)} fusion(bf16[1024,1024]{1,0:T(8,128)(2,1)S(1)} %convert_element_type.59, bf16[2048,1024]{1,0:T(8,128)(2,1)} %reshape.111), kind=kOutput, calls=%fused_computation.18 | convolution fusion | flops 4294967296 | bytes 14680064 | tf_op jit(solution)/shard_map/dot_general | solution.py:38
  41.0 9.2 %copy.24 = f32[2048,1024]{1,0:T(8,128)} copy(f32[2048,1024]{0,1:T(8,128)} %convolution_bitcast_fusion) | data formatting | bytes 16777216 | tf_op jit(solution)/shard_map/dot_general | solution.py:38
  50.2 4.8 %copy.38 = bf16[8,8,32,1024]{3,2,1,0:T(8,128)(2,1)S(1)} copy(bf16[8,8,32,1024]{3,1,2,0:T(8,128)(2,1)} %bitcast.44) | data formatting | bytes 8388608
  55.0 1.3 bitcast_add_fusion
  56.3 0.0 copy-start.4
  56.3 0.0 copy-start.5
  56.3 0.0 copy-start.6
  56.4 0.0 copy-start.2
  56.4 5.0 %copy.39 = f32[8,8,32,1024]{3,1,2,0:T(8,128)S(1)} copy(f32[8,8,32,1024]{3,2,1,0:T(8,128)S(1)} %bitcast.48) | data formatting | bytes 16777216
  61.5 3.5 fusion.8
  65.0 0.0 copy-start.3
  65.1 2.6 copy.41
  67.6 11.9 %all-to-all-start = ((bf16[64,128,256]{2,0,1:T(8,128)(2,1)}), bf16[64,128,256]{2,0,1:T(8,128)(2,1)}, u32[]{:S(2)}, u32[]{:S(2)}) async-start(bf16[64,128,256]{2,0,1:T(8,128)(2,1)} %bitcast.50), calls=%async_computation | async-start | bytes 8388608 | tf_op jit(solution)/shard_map/all_to_all | solution.py:53
  79.6 0.3 all-reduce.3.cloned.1.call-start
  79.9 0.1 copy.27
  80.0 0.2 reshape.117
  80.2 52.2 %all-to-all-done = bf16[64,128,256]{2,0,1:T(8,128)(2,1)} async-done(((bf16[64,128,256]{2,0,1:T(8,128)(2,1)}), bf16[64,128,256]{2,0,1:T(8,128)(2,1)}, u32[]{:S(2)}, u32[]{:S(2)}) %all-to-all-start) | async-done | bytes 4194336 | tf_op jit(solution)/shard_map/all_to_all | solution.py:53
  132.4 13.5 %gather_fusion = bf16[384,64,256]{2,1,0:T(8,128)(2,1)} fusion(bf16[128,64,256]{2,1,0:T(8,128)(2,1)} %bitcast.4, s32[1024]{0:T(1024)S(1)} %pad_clamp_fusion), kind=kCustom, calls=%fused_computation | custom fusion | bytes 25167360 | tf_op jit(solution)/shard_map/gather | solution.py:56
  145.9 12.7 %fusion.1 = f32[128,4,64,64]{3,2,1,0:T(8,128)} fusion(bf16[128,3,64,256]{3,2,1,0:T(8,128)(2,1)} %bitcast.53, bf16[128,1,64,256]{3,2,1,0:T(8,128)(2,1)} %bitcast.6, bf16[64,128,256]{2,0,1:T(8,128)(2,1)} %all-to-all-done), kind=kOutput, calls=%fused_computation.7 | convolution fusion | flops 1082130432 | bytes 29360128 | tf_op jit(solution)/shard_map/agc,akhc->akgh/dot_general | solution.py:58
  158.6 15.7 %copy.29 = f32[128,4,64,64]{0,2,3,1:T(8,128)} copy(f32[128,4,64,64]{3,2,1,0:T(8,128)} %fusion.1) | data formatting | bytes 16777216 | tf_op jit(solution)/shard_map/agc,akhc->akgh/dot_general | solution.py:58
  174.4 0.0 all-reduce.3.cloned.1.call-update
  174.4 157.1 %all-reduce.3.cloned.1.call-done = f32[128,4,64,64]{0,3,2,1:T(8,128)} async-done(((f32[128,4,64,64]{0,3,2,1:T(8,128)}), f32[128,4,64,64]{0,3,2,1:T(8,128)}) %all-reduce.3.cloned.1.call-update) | async-done | bytes 8388624 | tf_op jit(solution)/shard_map/psum | solution.py:66
  331.5 6.8 %multiply_convert_fusion = bf16[128,4,64,64]{0,3,2,1:T(8,128)(2,1)} fusion(f32[128,4,64,64]{0,3,2,1:T(8,128)} %all-reduce.3.cloned.1.call-done, f32[4,64,64]{2,1,0:T(8,128)S(1)} %pad_convert_fusion), kind=kLoop, calls=%fused_computation.16 | loop fusion | flops 8388608 | bytes 12648448 | tf_op jit(solution)/shard_map/convert_element_type | solution.py:67
  338.3 12.9 %copy.30 = bf16[128,4,64,64]{3,2,1,0:T(8,128)(2,1)} copy(bf16[128,4,64,64]{0,3,2,1:T(8,128)(2,1)} %multiply_convert_fusion) | data formatting | bytes 8388608 | tf_op jit(solution)/shard_map/convert_element_type | solution.py:67
  351.3 13.1 %fusion.7 = bf16[128,64,256]{2,1,0:T(8,128)(2,1)} fusion(bf16[128,4,64,64]{3,2,1,0:T(8,128)(2,1)} %copy.30, bf16[128,3,64,256]{3,2,1,0:T(8,128)(2,1)} %bitcast.54, bf16[128,1,64,256]{3,2,1,0:T(8,128)(2,1)} %bitcast.6, bf16[64,128,256]{2,0,1:T(8,128)(2,1)} %all-to-all-done), kind=kOutput, calls=%fused_computation.14 | convolution fusion | flops 1088421888 | bytes 29360128 | tf_op jit(solution)/shard_map/akgh,akhc->agc/dot_general | solution.py:68
  364.4 60.1 %all_to_all.32 = bf16[128,64,256]{2,1,0:T(8,128)(2,1)S(1)} all-to-all(bf16[128,64,256]{2,1,0:T(8,128)(2,1)} %fusion.7), channel_id=1, replica_groups=mesh['grid'=32,'rep'=4] {'grid','rep'}, dimensions={0} | all-to-all | bytes 8388608 | tf_op jit(solution)/shard_map/all_to_all | solution.py:71
  424.4 2.3 copy.37
  (18 shorter events, 0.1 us)
Async XLA Ops:
  50.2 4.8 %copy-start.1 = (f32[2048,1024]{1,0:T(8,128)S(1)}, f32[2048,1024]{1,0:T(8,128)}, u32[]{:S(2)}) copy-start(f32[2048,1024]{1,0:T(8,128)} %copy.24) | copy-start | bytes 25165828
  56.3 5.1 %copy-start.4 = (f32[64]{0:T(128)S(1)}, f32[64]{0:T(128)}, u32[]{:S(2)}) copy-start(f32[64]{0:T(128)} %param.10) | copy-start | bytes 772
  56.3 5.1 %copy-start.5 = (s32[64]{0:T(128)S(1)}, s32[64]{0:T(128)}, u32[]{:S(2)}) copy-start(s32[64]{0:T(128)} %param.11) | copy-start | bytes 772
  56.3 5.1 %copy-start.6 = (s32[64]{0:T(128)S(1)}, s32[64]{0:T(128)}, u32[]{:S(2)}) copy-start(s32[64]{0:T(128)} %param.12) | copy-start | bytes 772
  56.3 5.1 %copy-start = (bf16[64,32768]{1,0:T(8,128)(2,1)S(1)}, bf16[64,32768]{1,0:T(8,128)(2,1)}, u32[]{:S(2)}) copy-start(bf16[64,32768]{1,0:T(8,128)(2,1)} %param.7) | copy-start | bytes 12582916
  56.4 5.1 %copy-start.2 = (f32[32768]{0:T(1024)S(1)}, f32[32768]{0:T(1024)}, u32[]{:S(2)}) copy-start(f32[32768]{0:T(1024)} %param.9) | copy-start | bytes 393220
  65.0 14.8 %copy-start.3 = (s32[128,3]{0,1:T(4,128)S(1)}, s32[128,3]{0,1:T(4,128)}, u32[]{:S(2)}) copy-start(s32[128,3]{0,1:T(4,128)} %param.13) | copy-start | bytes 4612
  67.6 64.8 %all-to-all-start = ((bf16[64,128,256]{2,0,1:T(8,128)(2,1)}), bf16[64,128,256]{2,0,1:T(8,128)(2,1)}, u32[]{:S(2)}, u32[]{:S(2)}) async-start(bf16[64,128,256]{2,0,1:T(8,128)(2,1)} %bitcast.50), calls=%async_computation | async-start | bytes 8388608 | tf_op jit(solution)/shard_map/all_to_all | solution.py:53
  79.6 251.9 %all-reduce.3.cloned.1.call-start = ((), (), s32[]{:S(2)}) async-start(), calls=%async_computation.2 | async-start | bytes 16777216 | tf_op jit(solution)/shard_map/psum | solution.py:66
Sparse Core Ops, SparseCore 0:
  174.5 156.9 all-reduce.2
where the time goes:
time: 435 us; the launch traced here: 434 us
  waiting for transfers between devices  209 us (48%)
  local copies, waits for them, and re-layouts  85.2 us (20%)
  blocking collectives  60.1 us (14%)
  matrix products  36.1 us (8%)
  other arithmetic  17.1 us (4%)
  between operations  13.6 us (3%)
  starting transfers between devices  12.2 us (3%)
    psum x1, waiting for transfers between devices, on_device(): summed = lax.psum(local_intersection, ('grid', 'rep'))  157 us
    all_to_all x1, blocking collectives, on_device(): lax.all_to_all(result_grid, ('grid', 'rep'), split_axis=0, concat_axis=1,...  60.1 us
    all_to_all x1, waiting for transfers between devices, on_device(): lax.all_to_all(refined, ('grid', 'rep'), split_axis=1, concat_axis=0, til...  52.2 us
    dot_general x1, local copies, waits for them, and re-layouts, on_device(): jnp.einsum('agc,akhc->akgh', grouped, stacked, preferred_element_type=jnp...  15.7 us
    gather x1, local copies, waits for them, and re-layouts, on_device(): partner_rows = grouped[partner_groups]  13.5 us
    dot_general x1, matrix products, on_device(): jnp.einsum('akgh,akhc->agc', coupling, stacked, preferred_element_type=jn...  13.1 us
    convert_element_type x1, local copies, waits for them, and re-layouts, on_device(): (0.5 * (summed * weight - identity_block[None])).astype(jnp.bfloat16)  12.9 us
    dot_general x1, matrix products, on_device(): jnp.einsum('agc,akhc->akgh', grouped, stacked, preferred_element_type=jnp...  12.7 us
  transfers between devices with their start and end apart: 2, of which 2 were waited for; matrix products, arithmetic and copies ran while one was open for 0% of the time, Pallas kernels for 0%

commit v1 on v0

v1 whole, which is shorter than its diff:
```python
import functools

import jax
import jax.numpy as jnp
from jax import lax
from jax.experimental import pallas as pl
from jax.experimental.pallas import tpu as pltpu
from jax.sharding import PartitionSpec as P

MESH = pl.DeviceIdType.MESH
SIDE = 32
NC = 32768
BLOCK = 64
GROUP = 64
TAPS = 16
LMAX = 384
FOLD = 384
Z, X, Y = 0, 1, 2
ORDERS = ((Z, X, Y), (X, Y, Z), (Y, Z, X))
F32 = jnp.float32
BF16 = jnp.bfloat16


def position():
    grid = lax.axis_index("grid")
    rep = lax.axis_index("rep")
    return [lax.div(grid, 8), lax.rem(lax.div(grid, 2), 4), rep], lax.rem(grid, 2)


def device_of(pos, core):
    return (pos[Z] * 8 + pos[X] * 2 + core, pos[Y])


def moved(pos, axis, step):
    out = list(pos)
    out[axis] = lax.rem(pos[axis] + step, 4)
    return out


def enter(pos, core):
    barrier = pltpu.get_barrier_semaphore()
    other = 1 - core
    peers = [device_of(pos, other)]
    for axis in (Z, X, Y):
        for step in (1, 2, 3):
            for c in (core, other):
                peers.append(device_of(moved(pos, axis, step), c))
    for peer in peers:
        pl.semaphore_signal(barrier, inc=1, device_id=peer, device_id_type=MESH)
    pl.semaphore_wait(barrier, len(peers))


def remote(src, dst, sems, index, device):
    return pltpu.make_async_remote_copy(
        src_ref=src,
        dst_ref=dst,
        send_sem=sems[0].at[index],
        recv_sem=sems[1].at[index],
        device_id=device,
        device_id_type=MESH,
    )


def stage_one(order, pos, core, src, dst, sems, base):
    axis = order[0]
    mine = pos[axis]
    copies = []
    for step in (1, 3, 2, 0):
        for flip in (0, 1):
            c = core if flip == 0 else 1 - core
            to = moved(pos, axis, step)
            index = base + step * 2 + flip
            if step == 0 and flip == 0:
                copies.append(
                    pltpu.make_async_copy(src.at[mine, core], dst.at[mine, core], sems[1].at[index])
                )
            else:
                copies.append(
                    remote(src.at[to[axis], c], dst.at[mine, core], sems, index, device_of(to, c))
                )
    for copy in copies:
        copy.start()
    return copies


def stage_two(order, pos, core, src, dst, sems, base):
    axis = order[1]
    mine = pos[axis]
    copies = []
    for step in (1, 3, 2, 0):
        to = moved(pos, axis, step)
        index = base + 8 + step
        if step == 0:
            copies.append(pltpu.make_async_copy(src.at[:, :, mine], dst.at[mine], sems[1].at[index]))
        else:
            copies.append(
                remote(src.at[:, :, to[axis]], dst.at[mine], sems, index, device_of(to, core))
            )
    for copy in copies:
        copy.start()
    return copies


def stage_three(order, pos, core, src, dst, sems, base):
    axis = order[2]
    mine = pos[axis]
    copies = []
    for step in (1, 3, 2, 0):
        to = moved(pos, axis, step)
        index = base + 12 + step
        if step == 0:
            copies.append(
                pltpu.make_async_copy(src.at[:, :, :, mine], dst.at[mine], sems[1].at[index])
            )
        else:
            copies.append(
                remote(src.at[:, :, :, to[axis]], dst.at[mine], sems, index, device_of(to, core))
            )
    for copy in copies:
        copy.start()
    return copies


def wait_all(copies):
    for copy in copies:
        copy.wait()


def place(order, z, x, y):
    pos = (z, x, y)
    return pos[order[0]], pos[order[1]], pos[order[2]]


def tap_of(distance, taps_ref):
    out = jnp.zeros(distance.shape, F32)
    for t in range(TAPS):
        out = jnp.where(distance == t, taps_ref[t], out)
    return out


def build_matrices(taps_ref, line_ref, plane_ref):
    rows = lax.broadcasted_iota(jnp.int32, (256, 256), 0)
    cols = lax.broadcasted_iota(jnp.int32, (256, 256), 1)
    same = (rows & 15) == (cols & 15)
    for shift in (-1, 0, 1):
        value = tap_of((cols >> 4) - (rows >> 4) + 16 * shift + TAPS // 2, taps_ref)
        value = jnp.where(same, value, 0.0).astype(BF16)
        if shift == 0:
            line_ref[0:256, 0:256] = value
            line_ref[256:512, 256:512] = value
        elif shift == 1:
            line_ref[0:256, 256:512] = value
        else:
            line_ref[256:512, 0:256] = value
    for shift in (-1, 0, 1):
        value = tap_of((rows >> 5) - (cols >> 5) + 8 * shift + TAPS // 2, taps_ref)
        value = jnp.where((rows & 31) == (cols & 31), value, 0.0)
        if shift == 0:
            inner = tap_of((rows & 31) - (cols & 31) + TAPS // 2, taps_ref)
            value = value + jnp.where((rows >> 5) == (cols >> 5), inner, 0.0)
        value = value.astype(BF16)
        nothing = jnp.zeros_like(value)
        for c in range(4):
            inside = 0 <= c + shift < 4
            plane_ref[c, (shift + 1) * 256 : (shift + 2) * 256, :] = value if inside else nothing


def refine_half(fh, cc, refs):
    fn_ref, params_ref, pot_ref, line_ref, plane_ref, acc_ref, r_ref, send = refs
    c0 = pl.multiple_of(cc * 256, 256)
    cm = pl.multiple_of(jnp.maximum(cc - 1, 0) * 256, 256)
    cp = pl.multiple_of(jnp.minimum(cc + 1, 3) * 256, 256)

    def stacked(f0, offset):
        return jnp.concatenate(
            [fn_ref[f0 : f0 + 16, pl.ds(pl.multiple_of(x * 1024 + offset, 256), 256)] for x in range(SIDE)],
            axis=0,
        )

    for fl in range(2):
        f0 = fh * 32 + fl * 16
        own = stacked(f0, c0)
        acc = jnp.dot(line_ref[...], own, preferred_element_type=F32)
        acc += jnp.dot(stacked(f0, cm), plane_ref[cc, 0:256, :], preferred_element_type=F32)
        acc += jnp.dot(own, plane_ref[cc, 256:512, :], preferred_element_type=F32)
        acc += jnp.dot(stacked(f0, cp), plane_ref[cc, 512:768, :], preferred_element_type=F32)
        acc_ref[fl] = acc

    lane_block = lax.broadcasted_iota(jnp.int32, (16, 256), 1) >> 6
    column = []
    for fl in range(2):
        f0 = fh * 32 + fl * 16
        energy = jnp.broadcast_to(params_ref[f0 : f0 + 16, 0:1], (16, 256))
        first = jnp.broadcast_to(params_ref[f0 : f0 + 16, 1:2], (16, 256)).astype(jnp.int32)
        last = jnp.broadcast_to(params_ref[f0 : f0 + 16, 2:3], (16, 256)).astype(jnp.int32)
        first = first - lane_block
        last = last - lane_block
        column.append((energy, 0.3 / (1.0 - energy), first, last))

    def refined(x, fl):
        f0 = fh * 32 + fl * 16
        energy, step, first, last = column[fl]
        at = pl.ds(pl.multiple_of(x * 1024 + c0, 256), 256)
        value = fn_ref[f0 : f0 + 16, at].astype(F32)
        kinetic = acc_ref[fl, pl.ds(x * 16, 16), :]
        potential = pot_ref[pl.ds(x, 1), pl.ds(c0, 256)]
        gradient = kinetic + (potential - energy) * value
        value = value - step * gradient
        block = x * 16 + cc * 4
        inside = (first <= block) & (last > block)
        value = jnp.where(inside, value, 0.0)
        r_ref[f0 : f0 + 16, at] = value.astype(BF16)
        return value

    low = lax.broadcasted_iota(jnp.int32, (16, 128), 1) < 64
    for xs in range(16):
        z, x = xs // 4, xs % 4
        for fl in range(2):
            value = refined(xs + 8, fl).astype(BF16)
            for h in range(2):
                a1, a2, a3 = place(ORDERS[fh], z, x, cc)
                send[fh][a1, h, a2, a3, fl * 16 : fl * 16 + 16, :] = value[:, h * 128 : h * 128 + 128]
    for xd in range(8):
        folded = [refined(xd, fl) + refined(xd + 24, fl) for fl in range(2)]
        for h in range(2):
            z, x = xd // 2, (xd % 2) * 2 + h
            a, b = (part[:, h * 128 : h * 128 + 128] for part in folded)
            a1, a2, a3 = place(ORDERS[2], z, x, cc)
            first = jnp.where(low, a, pltpu.roll(b, 64, 1))
            second = jnp.where(low, pltpu.roll(a, 64, 1), b)
            send[2][a1, 0, a2, a3, fh * 16 : fh * 16 + 16, :] = first.astype(BF16)
            send[2][a1, 1, a2, a3, fh * 16 : fh * 16 + 16, :] = second.astype(BF16)


def exchange_in(
    fn_hbm, taps_ref, params_ref, pot_ref, start_ref,
    g0, g1, g2, st_out, r_hbm, own_ref,
    fn_ref, line_ref, plane_ref, acc_ref, r_ref,
    s0, s1, s2, a0, a1, a2, b0, b1, b2, st_a, st_b,
    load_sem, store_sem, send_sem, recv_sem, ssend_sem, srecv_sem,
):
    pos, core = position()
    load = pltpu.make_async_copy(fn_hbm, fn_ref, load_sem)
    load.start()
    enter(pos, core)
    sems = (send_sem, recv_sem)
    ssems = (ssend_sem, srecv_sem)
    send, one, two, out = (s0, s1, s2), (a0, a1, a2), (b0, b1, b2), (g0, g1, g2)

    starts = []
    for step in range(4):
        for flip in range(2):
            c = core if flip == 0 else 1 - core
            index = step * 2 + flip
            dst = st_a.at[pos[Z], core]
            if index == 0:
                starts.append(pltpu.make_async_copy(start_ref, dst, srecv_sem.at[index]))
            else:
                to = device_of(moved(pos, Z, step), c)
                starts.append(remote(start_ref, dst, ssems, index, to))
    for copy in starts:
        copy.start()

    build_matrices(taps_ref, line_ref, plane_ref)
    load.wait()
    refs = (fn_ref, params_ref, pot_ref, line_ref, plane_ref, acc_ref, r_ref, send)
    flying = [None] * 3
    for fh in range(2):
        lax.fori_loop(0, 4, lambda cc, carry: (refine_half(fh, cc, refs), carry)[1], 0)
        flying[fh] = stage_one(ORDERS[fh], pos, core, send[fh], one[fh], sems, fh * 16)
    flying[2] = stage_one(ORDERS[2], pos, core, send[2], one[2], sems, 32)
    store = pltpu.make_async_copy(r_ref, r_hbm, store_sem)
    store.start()

    wait_all(starts)
    starts = []
    for step in range(4):
        dst = st_b.at[pos[X]]
        if step == 0:
            starts.append(pltpu.make_async_copy(st_a, dst, srecv_sem.at[8 + step]))
        else:
            starts.append(remote(st_a, dst, ssems, 8 + step, device_of(moved(pos, X, step), core)))
    for copy in starts:
        copy.start()

    def own_part(i, total):
        rows = r_ref[:, pl.ds(pl.multiple_of(i * 1024, 1024), 1024)]
        return total + lax.dot_general(
            rows, rows, (((1,), (1,)), ((), ())), preferred_element_type=F32
        )

    total = lax.fori_loop(0, NC // 1024, own_part, jnp.zeros((GROUP, GROUP), F32))
    unit = lax.broadcasted_iota(jnp.int32, (GROUP, GROUP), 0) == lax.broadcasted_iota(
        jnp.int32, (GROUP, GROUP), 1
    )
    own = 0.5 * (total * (1.0 / (BLOCK * LMAX)) - jnp.where(unit, 1.0, 0.0))
    own_ref[...] = own.astype(BF16)

    wait_all(starts)
    starts = []
    for step in range(4):
        dst = st_out.at[pos[Y]]
        if step == 0:
            starts.append(pltpu.make_async_copy(st_b, dst, srecv_sem.at[12 + step]))
        else:
            starts.append(remote(st_b, dst, ssems, 12 + step, device_of(moved(pos, Y, step), core)))
    for copy in starts:
        copy.start()

    for t in range(3):
        wait_all(flying[t])
        flying[t] = stage_two(ORDERS[t], pos, core, one[t], two[t], sems, t * 16)
    for t in range(3):
        wait_all(flying[t])
        flying[t] = stage_three(ORDERS[t], pos, core, two[t], out[t], sems, t * 16)
    for t in range(3):
        wait_all(flying[t])
    wait_all(starts)
    store.wait()


def run_exchange_in(functions, filter_taps, potential, energies, region_start, region_length):
    params = jnp.stack(
        [energies, region_start.astype(F32), (region_start + region_length).astype(F32)], axis=1
    )
    starts = jnp.pad(region_start.astype(F32), (0, 64)).reshape(1, 128)
    vmem = pl.BlockSpec(memory_space=pltpu.VMEM)
    anywhere = pl.BlockSpec(memory_space=pltpu.HBM)
    piece = jax.ShapeDtypeStruct((4, 4, 4, 2, 32, 128), BF16)
    return pl.pallas_call(
        exchange_in,
        out_shape=(
            piece, piece, piece,
            jax.ShapeDtypeStruct((4, 4, 4, 2, 1, 128), F32),
            jax.ShapeDtypeStruct((GROUP, NC), BF16),
            jax.ShapeDtypeStruct((GROUP, GROUP), BF16),
        ),
        in_specs=[anywhere, pl.BlockSpec(memory_space=pltpu.SMEM), vmem, vmem, vmem],
        out_specs=(anywhere, anywhere, anywhere, anywhere, anywhere, vmem),
        scratch_shapes=[
            pltpu.VMEM((GROUP, NC), BF16),
            pltpu.VMEM((512, 512), BF16),
            pltpu.VMEM((4, 768, 256), BF16),
            pltpu.VMEM((2, 512, 256), F32),
            pltpu.VMEM((GROUP, NC), BF16),
        ]
        + [pltpu.VMEM((4, 2, 4, 4, 32, 128), BF16)] * 3
        + [pltpu.VMEM((4, 2, 4, 4, 32, 128), BF16)] * 3
        + [pltpu.VMEM((4, 4, 2, 4, 32, 128), BF16)] * 3
        + [
            pltpu.VMEM((4, 2, 1, 128), F32),
            pltpu.VMEM((4, 4, 2, 1, 128), F32),
            pltpu.SemaphoreType.DMA,
            pltpu.SemaphoreType.DMA,
            pltpu.SemaphoreType.DMA((48,)),
            pltpu.SemaphoreType.DMA((48,)),
            pltpu.SemaphoreType.DMA((16,)),
            pltpu.SemaphoreType.DMA((16,)),
        ],
        compiler_params=pltpu.CompilerParams(
            collective_id=0, has_side_effects=True, vmem_limit_bytes=60 * 1024 * 1024
        ),
    )(
        functions,
        filter_taps.astype(F32),
        params,
        potential.reshape(SIDE, SIDE * SIDE),
        starts,
    )


def unpack_halves(piece):
    low = lax.broadcasted_iota(jnp.int32, (16, 128), 1) < 64
    parts = []
    for fh in range(2):
        p = piece[fh * 16 : fh * 16 + 16].astype(F32)
        q = pltpu.roll(p, 64, 1)
        parts.append(jnp.where(low, p, q))
        parts.append(jnp.where(low, q, p))
    return jnp.concatenate(parts, axis=0)


def split(g):
    return g >> 5, (g >> 3) & 3, (g >> 2) & 1, g & 3


def orthonormalize(
    partners_ref, g0_hbm, g1_hbm, g2_hbm, st_hbm,
    f0_hbm, f1_hbm, f2_hbm,
    g0, g1, g2, st_ref, rows_ref, after_ref, u_ref,
    q0, q1, q2, p0, p1, p2, m0, m1, m2, t0, t1, t2, n0, n1, n2, v0, v1, v2,
    k0, k1, k2, l0, l1, l2, c0, c1, c2,
    s0, s1, s2, a0, a1, a2, b0, b1, b2,
    load_sem, r_send, r_recv, g_send, g_recv, x_send, x_recv, o_send, o_recv,
):
    pos, core = position()
    loads = [
        pltpu.make_async_copy(src, dst, load_sem.at[i])
        for i, (src, dst) in enumerate(((g0_hbm, g0), (g1_hbm, g1), (g2_hbm, g2), (st_hbm, st_ref)))
    ]
    for copy in loads:
        copy.start()
    enter(pos, core)
    wait_all(loads)
    orders = ORDERS

    for i in range(128):
        y, x, z, c = i >> 5, (i >> 3) & 3, (i >> 1) & 3, i & 1
        rows_ref[z * 32 + x * 8 + c * 4 + y : z * 32 + x * 8 + c * 4 + y + 1, :] = st_ref[y, x, z, c]
    block = (pos[Z] * 2 + lax.div(pos[X], 2)) * 16 + pos[Y] * 4 + lax.rem(pos[X], 2) * 2 + core
    above = jnp.where(rows_ref[...] > block.astype(F32), 1.0, 0.0)
    after_ref[...] = jnp.transpose(above)[0:GROUP]

    lower = lax.broadcasted_iota(jnp.int32, (GROUP, 128), 1) < 64

    def unfold(g, carry):
        z, x, c, y = split(g)
        u_ref[g, 0:32, 0:128] = g0[y, x, z, c]
        u_ref[g, 32:64, 0:128] = g1[z, y, x, c]
        folded = unpack_halves(g2[x, z, y, c])
        turned = pltpu.roll(after_ref[...], lax.rem(128 - g, 128), 1)
        upper = jnp.broadcast_to(turned[:, 0:1], (GROUP, 128)) > 0.5
        keep = jnp.logical_xor(upper, lower)
        u_ref[g, :, 128:256] = jnp.where(keep, folded, 0.0).astype(BF16)
        return carry

    lax.fori_loop(0, 128, unfold, 0, unroll=2)

    q, p, m = (q0, q1, q2), (p0, p1, p2), (m0, m1, m2)
    t, n, v = (t0, t1, t2), (n0, n1, n2), (v0, v1, v2)
    half_low = lax.broadcasted_iota(jnp.int32, (32, 128), 1) < 64

    def intersect(g, carry):
        z, x, c, y = split(g)
        rows = u_ref[g]
        others = jnp.concatenate([u_ref[partners_ref[g, k]] for k in range(3)], axis=0)
        part = lax.dot_general(rows, others, (((1,), (1,)), ((), ())), preferred_element_type=F32)
        q0[z, c, x, y] = part[0:32, 0:128].astype(BF16)
        q1[x, c, y, z] = part[32:64, 0:128].astype(BF16)
        last = jnp.concatenate([part[:, 128:192], part[:, 128:192]], axis=1)
        q2[y, c, z, x] = jnp.where(half_low, last[0:32], last[32:64]).astype(BF16)
        return carry

    lax.fori_loop(0, 128, intersect, 0, unroll=2)

    flying = [None] * 3
    for i in range(3):
        axis = orders[i][0]
        copies = []
        for step in range(4):
            for flip in range(2):
                if step == 0 and flip == 0:
                    continue
                cc = core if flip == 0 else 1 - core
                to = moved(pos, axis, step)
                index = step * 2 + flip
                copies.append(
                    remote(q[i].at[to[axis], cc], p[i].at[index - 1], (r_send, r_recv), i * 16 + index, device_of(to, cc))
                )
        for copy in copies:
            copy.start()
        flying[i] = copies
    for i in range(3):
        wait_all(flying[i])
        mine = pos[orders[i][0]]
        for j in range(4):
            total = q[i][mine, core, j].astype(F32)
            for k in range(7):
                total += p[i][k, j].astype(F32)
            m[i][j] = total.astype(BF16)
        axis = orders[i][1]
        copies = []
        for step in range(1, 4):
            to = moved(pos, axis, step)
            copies.append(
                remote(m[i].at[to[axis]], t[i].at[step - 1], (r_send, r_recv), i * 16 + 8 + step, device_of(to, core))
            )
        for copy in copies:
            copy.start()
        flying[i] = copies
    for i in range(3):
        wait_all(flying[i])
        total = m[i][pos[orders[i][1]]].astype(F32)
        for k in range(3):
            total += t[i][k].astype(F32)
        n[i][...] = total.astype(BF16)
        axis = orders[i][2]
        copies = []
        for step in range(1, 4):
            to = moved(pos, axis, step)
            copies.append(
                remote(n[i].at[to[axis]], v[i].at[step - 1], (r_send, r_recv), i * 16 + 12 + step, device_of(to, core))
            )
        for copy in copies:
            copy.start()
        flying[i] = copies

    kk, ll, cp = (k0, k1, k2), (l0, l1, l2), (c0, c1, c2)
    for i in range(3):
        wait_all(flying[i])
        mine = pos[orders[i][2]]
        total = n[i][mine].astype(F32)
        for k in range(3):
            total += v[i][k].astype(F32)
        kk[i][mine] = (0.5 * (total * (1.0 / (BLOCK * LMAX)))).astype(BF16)
        axis = orders[i][2]
        copies = [
            remote(kk[i].at[mine], kk[i].at[mine], (g_send, g_recv), i * 16 + step, device_of(moved(pos, axis, step), core))
            for step in range(1, 4)
        ]
        for copy in copies:
            copy.start()
        flying[i] = copies
    for i in range(3):
        wait_all(flying[i])
        axis = orders[i][1]
        mine = pos[axis]
        copies = [pltpu.make_async_copy(kk[i], ll[i].at[mine], g_recv.at[i * 16 + 4])]
        for step in range(1, 4):
            copies.append(
                remote(kk[i], ll[i].at[mine], (g_send, g_recv), i * 16 + 4 + step, device_of(moved(pos, axis, step), core))
            )
        for copy in copies:
            copy.start()
        flying[i] = copies
    for i in range(3):
        wait_all(flying[i])
        axis = orders[i][0]
        mine = pos[axis]
        copies = [pltpu.make_async_copy(ll[i], cp[i].at[mine, core], g_recv.at[i * 16 + 8])]
        for step in range(1, 4):
            copies.append(
                remote(ll[i], cp[i].at[mine, core], (g_send, g_recv), i * 16 + 8 + step, device_of(moved(pos, axis, step), core))
            )
        for copy in copies:
            copy.start()
        flying[i] = copies
    passed = []
    for i in range(3):
        axis = orders[i][0]
        for step in range(4):
            flying[i][step].wait()
            at = lax.rem(pos[axis] + 4 - step, 4)
            copy = remote(cp[i].at[at, core], cp[i].at[at, core], (x_send, x_recv), i * 4 + step, device_of(pos, 1 - core))
            copy.start()
            passed.append(copy)
    wait_all(passed)

    s = (s0, s1, s2)

    def shift(g, carry):
        z, x, c, y = split(g)
        others = jnp.concatenate([u_ref[partners_ref[g, k]] for k in range(3)], axis=0)
        third = c2[y, c, z, x]
        third = jnp.concatenate([third[:, 0:64], third[:, 64:128]], axis=0)
        pair = jnp.concatenate([c0[z, c, x, y], c1[x, c, y, z]], axis=0)
        weights = jnp.concatenate([pair, third], axis=1)
        moved_by = jnp.dot(weights, others, preferred_element_type=F32).astype(BF16)
        s0[z, c, x, y] = moved_by[0:48, 0:128]
        s1[x, c, y, z] = moved_by[0:48, 128:256]
        s2[y, c, z, x, 0:16] = moved_by[48:64, 0:128]
        s2[y, c, z, x, 16:32] = moved_by[48:64, 128:256]
        return carry

    lax.fori_loop(0, 128, shift, 0, unroll=2)

    one, two, out = (a0, a1, a2), (b0, b1, b2), (f0_hbm, f1_hbm, f2_hbm)
    sems = (o_send, o_recv)
    for i in range(3):
        flying[i] = stage_one(orders[i], pos, core, s[i], one[i], sems, i * 16)
    for i in range(3):
        wait_all(flying[i])
        flying[i] = stage_two(orders[i], pos, core, one[i], two[i], sems, i * 16)
    for i in range(3):
        wait_all(flying[i])
        flying[i] = stage_three(orders[i], pos, core, two[i], out[i], sems, i * 16)
    for i in range(3):
        wait_all(flying[i])


ROWS = (48, 48, 32)


def run_orthonormalize(partner_groups, g0, g1, g2, starts):
    anywhere = pl.BlockSpec(memory_space=pltpu.HBM)
    dma = pltpu.SemaphoreType.DMA

    def vmem(*shape):
        return pltpu.VMEM(shape, BF16)

    return pl.pallas_call(
        orthonormalize,
        out_shape=tuple(jax.ShapeDtypeStruct((4, 4, 4, 2, r, 128), BF16) for r in ROWS),
        in_specs=[pl.BlockSpec(memory_space=pltpu.SMEM)] + [anywhere] * 4,
        out_specs=(anywhere,) * 3,
        scratch_shapes=[vmem(4, 4, 4, 2, 32, 128)] * 3
        + [pltpu.VMEM((4, 4, 4, 2, 1, 128), F32), pltpu.VMEM((128, 128), F32), pltpu.VMEM((GROUP, 128), F32)]
        + [vmem(128, GROUP, 256)]
        + [vmem(4, 2, 4, 4, 32, 128)] * 3
        + [vmem(7, 4, 4, 32, 128)] * 3
        + [vmem(4, 4, 32, 128)] * 3
        + [vmem(3, 4, 32, 128)] * 3
        + [vmem(4, 32, 128)] * 3
        + [vmem(3, 32, 128)] * 3
        + [vmem(4, 32, 128)] * 3
        + [vmem(4, 4, 32, 128)] * 3
        + [vmem(4, 2, 4, 4, 32, 128)] * 3
        + [vmem(4, 2, 4, 4, r, 128) for r in ROWS]
        + [vmem(4, 2, 4, 4, r, 128) for r in ROWS]
        + [vmem(4, 4, 2, 4, r, 128) for r in ROWS]
        + [dma((4,)), dma((48,)), dma((48,)), dma((48,)), dma((48,)), dma((12,)), dma((12,)), dma((48,)), dma((48,))],
        compiler_params=pltpu.CompilerParams(
            collective_id=1, has_side_effects=True, vmem_limit_bytes=60 * 1024 * 1024
        ),
    )(partner_groups, g0, g1, g2, starts)


def finish(own_ref, r_hbm, f0_hbm, f1_hbm, f2_hbm, o_hbm, r_ref, f0_ref, f1_ref, f2_ref, o_ref, in_sem, out_sem):
    weights = own_ref[...]
    low = lax.broadcasted_iota(jnp.int32, (GROUP, 128), 1) < 64

    def loads(i):
        z, x = lax.div(i, 2), lax.rem(i, 2) * 2
        pairs = []
        for k, (slab, count) in enumerate(((i, 1), (i + 24, 1), (8 + 2 * i, 2))):
            cut = pl.ds(pl.multiple_of(slab * 1024, 1024), count * 1024)
            pairs.append((r_hbm.at[:, cut], r_ref.at[:, cut]))
        cut = pl.ds(x, 2)
        pairs.append((f0_hbm.at[:, cut, z], f0_ref.at[:, cut, z]))
        pairs.append((f1_hbm.at[z, :, cut], f1_ref.at[z, :, cut]))
        pairs.append((f2_hbm.at[cut, z], f2_ref.at[cut, z]))
        return [pltpu.make_async_copy(a, b, in_sem.at[i, k]) for k, (a, b) in enumerate(pairs)]

    def stores(i):
        out = []
        for k, (slab, count) in enumerate(((i, 1), (i + 24, 1), (8 + 2 * i, 2))):
            cut = pl.ds(pl.multiple_of(slab * 1024, 1024), count * 1024)
            out.append(pltpu.make_async_copy(o_ref.at[:, cut], o_hbm.at[:, cut], out_sem.at[i, k]))
        return out

    def each(make):
        def body(i, carry):
            for copy in make(i):
                copy.start()
            return carry

        return body

    lax.fori_loop(0, 8, each(loads), 0)

    def slab_part(slab, y, h, moved_by):
        at = pl.ds(pl.multiple_of(slab * 1024 + y * 256 + h * 128, 128), 128)
        rows = r_ref[:, at]
        shifted = jnp.dot(weights, rows, preferred_element_type=F32)
        o_ref[:, at] = (rows.astype(F32) - shifted - moved_by).astype(BF16)

    def step(i, carry):
        for copy in loads(i):
            copy.wait()
        z, x0 = lax.div(i, 2), lax.rem(i, 2) * 2
        for dx in range(2):
            x = x0 + dx
            for y in range(4):
                twos = []
                for c in range(2):
                    tail = f2_ref[x, z, y, c].astype(F32)
                    single = jnp.concatenate([f0_ref[y, x, z, c].astype(F32), tail[0:16]], axis=0)
                    slab_part(8 + 2 * i + dx, y, c, single)
                    twos.append(jnp.concatenate([f1_ref[z, y, x, c].astype(F32), tail[16:32]], axis=0))
                slab_part(i, y, dx, jnp.where(low, twos[0], pltpu.roll(twos[1], 64, 1)))
                slab_part(i + 24, y, dx, jnp.where(low, pltpu.roll(twos[0], 64, 1), twos[1]))
        for copy in stores(i):
            copy.start()
        return carry

    lax.fori_loop(0, 8, step, 0)

    def last(i, carry):
        for copy in stores(i):
            copy.wait()
        return carry

    lax.fori_loop(0, 8, last, 0)


def run_finish(own, refined, f0, f1, f2):
    anywhere = pl.BlockSpec(memory_space=pltpu.HBM)
    return pl.pallas_call(
        finish,
        out_shape=jax.ShapeDtypeStruct((GROUP, NC), BF16),
        in_specs=[pl.BlockSpec(memory_space=pltpu.VMEM)] + [anywhere] * 4,
        out_specs=anywhere,
        scratch_shapes=[pltpu.VMEM((GROUP, NC), BF16)]
        + [pltpu.VMEM((4, 4, 4, 2, r, 128), BF16) for r in ROWS]
        + [pltpu.VMEM((GROUP, NC), BF16), pltpu.SemaphoreType.DMA((8, 6)), pltpu.SemaphoreType.DMA((8, 3))],
        compiler_params=pltpu.CompilerParams(vmem_limit_bytes=40 * 1024 * 1024),
    )(own, refined, f0, f1, f2)


def on_device(functions, filter_taps, potential, energies, region_start, region_length, partner_groups):
    g0, g1, g2, starts, refined, own = run_exchange_in(
        functions, filter_taps, potential, energies, region_start, region_length
    )
    f0, f1, f2 = run_orthonormalize(partner_groups, g0, g1, g2, starts)
    return run_finish(own, refined, f0, f1, f2)


def solution(mesh):
    return jax.shard_map(
        on_device,
        mesh=mesh,
        in_specs=(
            P(("grid", "rep"), None),
            P(),
            P(),
            P(("grid", "rep")),
            P(("grid", "rep")),
            P(("grid", "rep")),
            P(),
        ),
        out_specs=P(("grid", "rep"), None),
        check_vma=False,
    )
```

time: 435 us -> 228 us (0.52)
  Pallas kernels: 0 us -> 213 us
  waiting for transfers between devices: 209 us -> 0 us
  local copies, waits for them, and re-layouts: 85.2 us -> 11.1 us
  blocking collectives: 60.1 us -> 0 us
  matrix products: 36.1 us -> 0 us
  other arithmetic: 17.1 us -> 2.54 us
  between operations: 13.6 us -> 0.03 us
  starting transfers between devices: 12.2 us -> 0 us
    pallas_call x0 -> x3, Pallas kernels: none -> 213 us  [the longest x1 143 us: run_orthonormalize(): pl.pallas_call(orthonormalize, out_shape=tuple((jax.ShapeDtypeStruct((4,...]
    psum x1 -> x0, waiting for transfers between devices: 157 us -> none  [on_device(): summed = lax.psum(local_intersection, ('grid', 'rep'))]
    all_to_all x1 -> x0, blocking collectives: 60.1 us -> none  [on_device(): lax.all_to_all(result_grid, ('grid', 'rep'), split_axis=0, concat_axis=1,...]
    all_to_all x1 -> x0, waiting for transfers between devices: 52.2 us -> none  [on_device(): lax.all_to_all(refined, ('grid', 'rep'), split_axis=1, concat_axis=0, til...]
    dot_general x4 -> x0, matrix products: 36.1 us -> none  [the longest x1 13.1 us: on_device(): jnp.einsum('akgh,akhc->agc', coupling, stacked, preferred_element_type=jn...]
    dot_general x2 -> x0, local copies, waits for them, and re-layouts: 25 us -> none  [the longest x1 15.7 us: on_device(): jnp.einsum('agc,akhc->akgh', grouped, stacked, preferred_element_type=jnp...]
    convert_element_type x2 -> x0, local copies, waits for them, and re-layouts: 24.3 us -> none  [the longest x1 12.9 us: on_device(): (0.5 * (summed * weight - identity_block[None])).astype(jnp.bfloat16)]
    convert_element_type x5 -> x2, other arithmetic: 16.9 us -> 1.87 us  [the longest x1 1.14 us: run_exchange_in(): filter_taps.astype(F32)]
  transfers between devices with their start and end apart: 2 -> 0, of which waited for: 2 -> 0; matrix products, arithmetic and copies ran while one was open for 0% -> 0% of each run, Pallas kernels for 0% -> 0%
where the time goes in v1:
time: 228 us; the launch traced here: 227 us
  Pallas kernels  213 us (93%)
  local copies, waits for them, and re-layouts  11.1 us (5%)
  other arithmetic  2.54 us (1%)
    pallas_call x1, Pallas kernels, run_orthonormalize(): pl.pallas_call(orthonormalize, out_shape=tuple((jax.ShapeDtypeStruct((4,...  143 us
    pallas_call x1, Pallas kernels, run_exchange_in(): pl.pallas_call(exchange_in, out_shape=(piece, piece, piece, jax.ShapeDtyp...  62.9 us
    unnamed x11, local copies, waits for them, and re-layouts  8.34 us
    pallas_call x1, Pallas kernels, run_finish(): pl.pallas_call(finish, out_shape=jax.ShapeDtypeStruct((GROUP, NC), BF16),...  7.25 us

profile of v1, /device:TPU:1, one launch (start us, length us, event | category | flops | bytes accessed | tf_op | source)
XLA Modules:
  0.0 227.1 jit_solution(18037134816157122320)
XLA Ops:
  0.0 1.1 convert_element_type.12.taps_ref
  1.1 0.7 fusion
  1.9 0.5 pad_bitcast_fusion.start_ref
  2.4 0.7 pad_maximum_fusion
  3.1 0.7 copy.12.params_ref
  3.8 1.4 copy.13.partners_ref
  5.2 1.6 reshape.6.pot_ref
  6.8 62.9 %shard_map.73 = (bf16[4,4,4,2,32,128]{5,4,3,2,1,0:T(8,128)(2,1)}, bf16[4,4,4,2,32,128]{5,4,3,2,1,0:T(8,128)(2,1)}, bf16[4,4,4,2,32,128]{5,4,3,2,1,0:T(8,128)(2,1...) custom-call(bf16[64,32768]{1,0:T(8,128)(2,1)} %fn_hbm.1, ...), custom_call_target="tpu_custom_call" | custom-call | tf_op jit(solution)/shard_map/pallas_call | solution.py:330
  69.6 143.3 %shard_map.74 = (bf16[4,4,4,2,48,128]{5,4,3,2,1,0:T(8,128)(2,1)}, bf16[4,4,4,2,48,128]{5,4,3,2,1,0:T(8,128)(2,1)}, bf16[4,4,4,2,32,128]{5,4,3,2,1,0:T(8,128)(2,1)}) custom-call(s32[128,3]{1,0:T(8,128)} %copy.13.partners_ref, bf16[4,4,4,2,32,128]{5,4,3,2,1,0:T(8,128)(2,1)} %get-tuple-element.16.g0_hbm, ...), custom_call_target="tpu_custom_call" | custom-call | tf_op jit(solution)/shard_map/pallas_call | solution.py:591
  212.9 0.0 copy-start
  213.0 2.2 copy-done
  215.1 0.0 copy-start.1
  215.1 1.4 copy-done.1
  216.5 0.0 copy-start.2
  216.5 1.4 copy-done.2
  217.9 0.0 copy-start.3
  218.0 1.2 copy-done.3
  219.2 0.0 copy-start.4
  219.2 0.7 copy-done.4
  219.9 7.2 %shard_map.75 = bf16[64,32768]{1,0:T(8,128)(2,1)} custom-call(bf16[64,64]{1,0:T(8,128)(2,1)S(1)} %copy-done.4, bf16[64,32768]{1,0:T(8,128)(2,1)S(1)} %copy-done, bf16[4,4,4,2,48,128]{5,4,3,2,1,0:T(8,128)(2,1)S(1)} %copy-done.1, bf16[4,4,4,2,48,128]{5,4,3,2,1,0:T(8,128)(2,1)S(1)} %copy-done.2, bf16[4,4,4,2,32,128]{5,4,3,2,1,0:T(8,128)(2,1)S(1)} %copy-done.3), custom_call_target="tpu_custom_call" | custom-call | tf_op jit(solution)/shard_map/pallas_call | solution.py:688
Async XLA Ops:
  212.9 2.2 copy-start
  215.1 1.4 copy-start.1
  216.5 1.4 copy-start.2
  217.9 1.2 copy-start.3
  219.2 0.7 copy-start.4

commit v2 on v1

v2 whole, which is shorter than its diff:
```python
import functools

import jax
import jax.numpy as jnp
from jax import lax
from jax.experimental import pallas as pl
from jax.experimental.pallas import tpu as pltpu
from jax.sharding import PartitionSpec as P

MESH = pl.DeviceIdType.MESH
SIDE = 32
NC = 32768
BLOCK = 64
GROUP = 64
TAPS = 16
LMAX = 384
FOLD = 384
Z, X, Y = 0, 1, 2
ORDERS = ((Z, X, Y), (X, Y, Z), (Y, Z, X))
F32 = jnp.float32
BF16 = jnp.bfloat16


def position():
    grid = lax.axis_index("grid")
    rep = lax.axis_index("rep")
    return [lax.div(grid, 8), lax.rem(lax.div(grid, 2), 4), rep], lax.rem(grid, 2)


def device_of(pos, core):
    return (pos[Z] * 8 + pos[X] * 2 + core, pos[Y])


def moved(pos, axis, step):
    out = list(pos)
    out[axis] = lax.rem(pos[axis] + step, 4)
    return out


def enter(pos, core):
    barrier = pltpu.get_barrier_semaphore()
    other = 1 - core
    peers = [device_of(pos, other)]
    for axis in (Z, X, Y):
        for step in (1, 2, 3):
            for c in (core, other):
                peers.append(device_of(moved(pos, axis, step), c))
    for peer in peers:
        pl.semaphore_signal(barrier, inc=1, device_id=peer, device_id_type=MESH)
    pl.semaphore_wait(barrier, len(peers))


def remote(src, dst, sems, index, device):
    return pltpu.make_async_remote_copy(
        src_ref=src,
        dst_ref=dst,
        send_sem=sems[0].at[index],
        recv_sem=sems[1].at[index],
        device_id=device,
        device_id_type=MESH,
    )


def part_of(pos, i):
    return lax.rem(pos[Y] + 1 + i, 4)


def stage_one(t, pos, core, src, dst, sems, i):
    axis = ORDERS[t][0]
    mine = pos[axis]
    yy = part_of(pos, i)
    remotes, local = [], None
    for step in (1, 3, 2, 0):
        for flip in (0, 1):
            c = core if flip == 0 else 1 - core
            to = moved(pos, axis, step)
            index = t * 40 + i * 8 + step * 2 + flip
            if t == 0:
                a, b = src.at[to[axis], c, :, yy], dst.at[mine, core, :, yy]
            else:
                a, b = src.at[to[axis], c, yy], dst.at[mine, core, yy]
            if step == 0 and flip == 0:
                local = pltpu.make_async_copy(a, b, sems[1].at[index])
            else:
                remotes.append(remote(a, b, sems, index, device_of(to, c)))
    return remotes + [local]


def stage_one_y(pos, core, src, dst, sems, step, flips=(0, 1)):
    mine = pos[Y]
    to = moved(pos, Y, step)
    out = []
    for flip in flips:
        c = core if flip == 0 else 1 - core
        out.append(
            remote(src.at[to[Y], c], dst.at[mine, core], sems, 80 + step * 2 + flip, device_of(to, c))
        )
    return out


def keep_y(pos, core, src, dst, sems):
    return pltpu.make_async_copy(src.at[pos[Y], core], dst.at[pos[Y], core], sems[1].at[80])


def start_part(pos, core, src, dst, sems, i):
    for t in (0, 1):
        for copy in stage_one(t, pos, core, src[t], dst[t], sems, i):
            copy.start()

    @pl.when(i < 3)
    def _():
        for copy in stage_one_y(pos, core, src[2], dst[2], sems, i + 1):
            copy.start()

    @pl.when(i == 3)
    def _():
        stage_one_y(pos, core, src[2], dst[2], sems, 0, (1,))[0].start()
        keep_y(pos, core, src[2], dst[2], sems).start()


def wait_one(t, pos, core, src, dst, sems):
    if t < 2:
        def body(i, carry):
            wait_all(stage_one(t, pos, core, src[t], dst[t], sems, i))
            return carry

        lax.fori_loop(0, 4, body, 0)
    else:
        for step in range(1, 4):
            wait_all(stage_one_y(pos, core, src[2], dst[2], sems, step))
        stage_one_y(pos, core, src[2], dst[2], sems, 0, (1,))[0].wait()
        keep_y(pos, core, src[2], dst[2], sems).wait()


def stage_two(t, pos, core, src, dst, sems):
    axis = ORDERS[t][1]
    mine = pos[axis]
    copies = []
    for step in (1, 3, 2, 0):
        to = moved(pos, axis, step)
        index = 120 + t * 8 + step
        if step == 0:
            copies.append(pltpu.make_async_copy(src.at[:, :, mine], dst.at[mine], sems[1].at[index]))
        else:
            copies.append(remote(src.at[:, :, to[axis]], dst.at[mine], sems, index, device_of(to, core)))
    for copy in copies:
        copy.start()
    return copies


def stage_three(t, pos, core, src, dst, sems):
    axis = ORDERS[t][2]
    mine = pos[axis]
    copies = []
    for step in (1, 3, 2, 0):
        to = moved(pos, axis, step)
        index = 120 + t * 8 + 4 + step
        if step == 0:
            copies.append(pltpu.make_async_copy(src.at[:, :, :, mine], dst.at[mine], sems[1].at[index]))
        else:
            copies.append(
                remote(src.at[:, :, :, to[axis]], dst.at[mine], sems, index, device_of(to, core))
            )
    for copy in copies:
        copy.start()
    return copies


SEMS = 144


def wait_all(copies):
    for copy in copies:
        copy.wait()


def place(order, z, x, y):
    pos = (z, x, y)
    return pos[order[0]], pos[order[1]], pos[order[2]]


def tap_of(distance, taps_ref):
    taps = taps_ref[...].astype(F32)
    out = jnp.zeros(distance.shape, F32)
    for t in range(TAPS):
        out = jnp.where(distance == t, jnp.broadcast_to(taps[:, t : t + 1], distance.shape), out)
    return out


def build_matrices(taps_ref, line_ref, plane_ref):
    rows = lax.broadcasted_iota(jnp.int32, (256, 256), 0)
    cols = lax.broadcasted_iota(jnp.int32, (256, 256), 1)
    same = (rows & 15) == (cols & 15)
    for shift in (-1, 0, 1):
        value = tap_of((cols >> 4) - (rows >> 4) + 16 * shift + TAPS // 2, taps_ref)
        value = jnp.where(same, value, 0.0).astype(BF16)
        if shift == 0:
            line_ref[0:256, 0:256] = value
            line_ref[256:512, 256:512] = value
        elif shift == 1:
            line_ref[0:256, 256:512] = value
        else:
            line_ref[256:512, 0:256] = value
    for shift in (-1, 0, 1):
        value = tap_of((rows >> 5) - (cols >> 5) + 8 * shift + TAPS // 2, taps_ref)
        value = jnp.where((rows & 31) == (cols & 31), value, 0.0)
        if shift == 0:
            inner = tap_of((rows & 31) - (cols & 31) + TAPS // 2, taps_ref)
            value = value + jnp.where((rows >> 5) == (cols >> 5), inner, 0.0)
        value = value.astype(BF16)
        nothing = jnp.zeros_like(value)
        for c in range(4):
            inside = 0 <= c + shift < 4
            plane_ref[c, (shift + 1) * 256 : (shift + 2) * 256, :] = value if inside else nothing


def refine_half(fh, cc, refs):
    fn_ref, params_ref, pot_ref, line_ref, plane_ref, acc_ref, r_ref, send = refs
    c0 = pl.multiple_of(cc * 256, 256)
    cm = pl.multiple_of(jnp.maximum(cc - 1, 0) * 256, 256)
    cp = pl.multiple_of(jnp.minimum(cc + 1, 3) * 256, 256)

    def stacked(f0, offset):
        return jnp.concatenate(
            [fn_ref[f0 : f0 + 16, pl.ds(pl.multiple_of(x * 1024 + offset, 256), 256)] for x in range(SIDE)],
            axis=0,
        )

    for fl in range(2):
        f0 = fh * 32 + fl * 16
        own = stacked(f0, c0)
        acc = jnp.dot(line_ref[...], own, preferred_element_type=F32)
        acc += jnp.dot(stacked(f0, cm), plane_ref[cc, 0:256, :], preferred_element_type=F32)
        acc += jnp.dot(own, plane_ref[cc, 256:512, :], preferred_element_type=F32)
        acc += jnp.dot(stacked(f0, cp), plane_ref[cc, 512:768, :], preferred_element_type=F32)
        acc_ref[fl] = acc

    lane_block = lax.broadcasted_iota(jnp.int32, (16, 256), 1) >> 6
    column = []
    for fl in range(2):
        f0 = fh * 32 + fl * 16
        energy = jnp.broadcast_to(params_ref[f0 : f0 + 16, 0:1], (16, 256))
        first = jnp.broadcast_to(params_ref[f0 : f0 + 16, 1:2], (16, 256)).astype(jnp.int32)
        last = jnp.broadcast_to(params_ref[f0 : f0 + 16, 2:3], (16, 256)).astype(jnp.int32)
        first = first - lane_block
        last = last - lane_block
        column.append((energy, 0.3 / (1.0 - energy), first, last))

    def refined(x, fl):
        f0 = fh * 32 + fl * 16
        energy, step, first, last = column[fl]
        at = pl.ds(pl.multiple_of(x * 1024 + c0, 256), 256)
        value = fn_ref[f0 : f0 + 16, at].astype(F32)
        kinetic = acc_ref[fl, pl.ds(x * 16, 16), :]
        row = x * 8 + cc * 2
        potential = jnp.concatenate([pot_ref[pl.ds(row, 1), :], pot_ref[pl.ds(row + 1, 1), :]], axis=1)
        gradient = kinetic + (potential - energy) * value
        value = value - step * gradient
        block = x * 16 + cc * 4
        inside = (first <= block) & (last > block)
        value = jnp.where(inside, value, 0.0)
        r_ref[f0 : f0 + 16, at] = value.astype(BF16)
        return value

    low = lax.broadcasted_iota(jnp.int32, (16, 128), 1) < 64
    for xs in range(16):
        z, x = xs // 4, xs % 4
        for fl in range(2):
            value = refined(xs + 8, fl).astype(BF16)
            for h in range(2):
                a1, a2, a3 = place(ORDERS[fh], z, x, cc)
                send[fh][a1, h, a2, a3, fl * 16 : fl * 16 + 16, :] = value[:, h * 128 : h * 128 + 128]
    for xd in range(8):
        folded = [refined(xd, fl) + refined(xd + 24, fl) for fl in range(2)]
        for h in range(2):
            z, x = xd // 2, (xd % 2) * 2 + h
            a, b = (part[:, h * 128 : h * 128 + 128] for part in folded)
            a1, a2, a3 = place(ORDERS[2], z, x, cc)
            first = jnp.where(low, a, pltpu.roll(b, 64, 1))
            second = jnp.where(low, pltpu.roll(a, 64, 1), b)
            send[2][a1, 0, a2, a3, fh * 16 : fh * 16 + 16, :] = first.astype(BF16)
            send[2][a1, 1, a2, a3, fh * 16 : fh * 16 + 16, :] = second.astype(BF16)


def unpack_halves(piece):
    low = lax.broadcasted_iota(jnp.int32, (16, 128), 1) < 64
    parts = []
    for fh in range(2):
        p = piece[fh * 16 : fh * 16 + 16].astype(F32)
        q = pltpu.roll(p, 64, 1)
        parts.append(jnp.where(low, p, q))
        parts.append(jnp.where(low, q, p))
    return jnp.concatenate(parts, axis=0)


def split(g):
    return g >> 5, (g >> 3) & 3, (g >> 2) & 1, g & 3


def orthonormalize(
    partners_ref, fn_hbm, taps_ref, energy_ref, start_ref, length_ref, pot_ref,
    f0_hbm, f1_hbm, f2_hbm, r_hbm, own_ref,
    fn_ref, line_ref, plane_ref, acc_ref, r_ref, square_ref, params_ref, first_ref,
    e0, e1, e2, a0, a1, a2, b0, b1, b2, g0, g1, g2, st_a, st_b, st_c,
    after_ref, u_ref,
    q0, q1, q2, p0, p1, p2, m0, m1, m2, t0, t1, t2, n0, n1, n2, v0, v1, v2,
    k0, k1, k2, l0, l1, l2, c0, c1, c2,
    s0, s1, s2, h0, h1, h2, i0, i1, i2,
    load_sem, store_sem, in_send, in_recv, st_send, st_recv, r_send, r_recv, g_send, g_recv, x_send, x_recv,
    o_send, o_recv,
):
    pos, core = position()
    load = pltpu.make_async_copy(fn_hbm, fn_ref, load_sem)
    load.start()
    enter(pos, core)

    first_ref[...] = jnp.zeros((1, 128), F32)
    first_ref[0:1, 0:GROUP] = start_ref[...].astype(F32)
    st_sems = (st_send, st_recv)
    starts = []
    for step in range(4):
        for flip in range(2):
            c = core if flip == 0 else 1 - core
            index = step * 2 + flip
            dst = st_a.at[pos[Z], core]
            if index == 0:
                starts.append(pltpu.make_async_copy(first_ref, dst, st_recv.at[index]))
            else:
                starts.append(remote(first_ref, dst, st_sems, index, device_of(moved(pos, Z, step), c)))

    square_ref[...] = jnp.zeros((128, 128), F32)
    square_ref[0:1, 0:GROUP] = energy_ref[...]
    square_ref[1:2, 0:GROUP] = start_ref[...].astype(F32)
    square_ref[2:3, 0:GROUP] = (start_ref[...] + length_ref[...]).astype(F32)
    params_ref[...] = jnp.transpose(square_ref[...])[0:GROUP]
    build_matrices(taps_ref, line_ref, plane_ref)
    for copy in starts:
        copy.start()
    load.wait()
    send, one, two, got = (e0, e1, e2), (a0, a1, a2), (b0, b1, b2), (g0, g1, g2)
    sems = (in_send, in_recv)
    refs = (fn_ref, params_ref, pot_ref, line_ref, plane_ref, acc_ref, r_ref, send)

    def refine(i, carry):
        for fh in range(2):
            refine_half(fh, part_of(pos, i), refs)
        start_part(pos, core, send, one, sems, i)
        return carry

    lax.fori_loop(0, 4, refine, 0)
    store = pltpu.make_async_copy(r_ref, r_hbm, store_sem)
    store.start()

    wait_all(starts)
    starts = []
    for step in range(4):
        dst = st_b.at[pos[X]]
        if step == 0:
            starts.append(pltpu.make_async_copy(st_a, dst, st_recv.at[8 + step]))
        else:
            starts.append(remote(st_a, dst, st_sems, 8 + step, device_of(moved(pos, X, step), core)))
    for copy in starts:
        copy.start()

    flying = [None] * 3
    for t in range(3):
        wait_one(t, pos, core, send, one, sems)
        flying[t] = stage_two(t, pos, core, one[t], two[t], sems)
    wait_all(starts)
    starts = []
    for step in range(4):
        dst = st_c.at[pos[Y]]
        if step == 0:
            starts.append(pltpu.make_async_copy(st_b, dst, st_recv.at[12 + step]))
        else:
            starts.append(remote(st_b, dst, st_sems, 12 + step, device_of(moved(pos, Y, step), core)))
    for copy in starts:
        copy.start()

    def own_part(i, total):
        rows = r_ref[:, pl.ds(pl.multiple_of(i * 1024, 1024), 1024)]
        return total + lax.dot_general(
            rows, rows, (((1,), (1,)), ((), ())), preferred_element_type=F32
        )

    total = lax.fori_loop(0, NC // 1024, own_part, jnp.zeros((GROUP, GROUP), F32))
    unit = lax.broadcasted_iota(jnp.int32, (GROUP, GROUP), 0) == lax.broadcasted_iota(
        jnp.int32, (GROUP, GROUP), 1
    )
    own = 0.5 * (total * (1.0 / (BLOCK * LMAX)) - jnp.where(unit, 1.0, 0.0))
    own_ref[...] = own.astype(BF16)

    for t in (2, 0, 1):
        wait_all(flying[t])
        flying[t] = stage_three(t, pos, core, two[t], got[t], sems)

    wait_all(starts)
    for i in range(128):
        y, x, z, c = i >> 5, (i >> 3) & 3, (i >> 1) & 3, i & 1
        square_ref[z * 32 + x * 8 + c * 4 + y : z * 32 + x * 8 + c * 4 + y + 1, :] = st_c[y, x, z, c]
    block = (pos[Z] * 2 + lax.div(pos[X], 2)) * 16 + pos[Y] * 4 + lax.rem(pos[X], 2) * 2 + core
    above = jnp.where(square_ref[...] > block.astype(F32), 1.0, 0.0)
    after_ref[...] = jnp.transpose(above)[0:GROUP]

    lower = lax.broadcasted_iota(jnp.int32, (GROUP, 128), 1) < 64

    for k in (3, 0, 1, 2):
        step = (1, 3, 2, 0)[k]
        flying[2][k].wait()
        x = lax.rem(pos[X] + 4 - step, 4)

        def unfold(j, carry, x=x):
            z, y, c = j >> 3, (j >> 1) & 3, j & 1
            g = z * 32 + x * 8 + c * 4 + y
            folded = unpack_halves(g2[x, z, y, c])
            turned = pltpu.roll(after_ref[...], lax.rem(128 - g, 128), 1)
            upper = jnp.broadcast_to(turned[:, 0:1], (GROUP, 128)) > 0.5
            keep = jnp.logical_xor(upper, lower)
            u_ref[g] = jnp.where(keep, folded, 0.0).astype(BF16)
            return carry

        lax.fori_loop(0, 32, unfold, 0, unroll=2)
    wait_all(flying[0])
    wait_all(flying[1])

    def columns(g):
        z, x, c, y = split(g)
        return jnp.concatenate(
            [jnp.concatenate([g0[y, x, z, c], g1[z, y, x, c]], axis=0), u_ref[g]], axis=1
        )

    def partners(g):
        return jnp.concatenate([columns(partners_ref[k, g]) for k in range(3)], axis=0)

    half_low = lax.broadcasted_iota(jnp.int32, (32, 128), 1) < 64
    q, p, m = (q0, q1, q2), (p0, p1, p2), (m0, m1, m2)
    t, n, v = (t0, t1, t2), (n0, n1, n2), (v0, v1, v2)
    sums = (r_send, r_recv)

    def intersect_part(i, carry):
        y = part_of(pos, i)

        def intersect(j, inner):
            z, x, c = j >> 3, (j >> 1) & 3, j & 1
            g = z * 32 + x * 8 + c * 4 + y
            part = lax.dot_general(
                columns(g), partners(g), (((1,), (1,)), ((), ())), preferred_element_type=F32
            )
            q0[z, c, x, y] = part[0:32, 0:128].astype(BF16)
            q1[x, c, y, z] = part[32:64, 0:128].astype(BF16)
            last = jnp.concatenate([part[:, 128:192], part[:, 128:192]], axis=1)
            q2[y, c, z, x] = jnp.where(half_low, last[0:32], last[32:64]).astype(BF16)
            return inner

        lax.fori_loop(0, 32, intersect, 0, unroll=2)
        start_part(pos, core, q, p, sums, i)
        return carry

    lax.fori_loop(0, 4, intersect_part, 0)

    orders = ORDERS
    for i in range(3):
        wait_one(i, pos, core, q, p, sums)
        for j in range(4):
            total = p[i][0, 0, j].astype(F32)
            for k in range(1, 8):
                total += p[i][k >> 1, k & 1, j].astype(F32)
            m[i][j] = total.astype(BF16)
        axis = orders[i][1]
        copies = []
        for step in range(1, 4):
            to = moved(pos, axis, step)
            copies.append(
                remote(m[i].at[to[axis]], t[i].at[step - 1], sums, 120 + i * 8 + step, device_of(to, core))
            )
        for copy in copies:
            copy.start()
        flying[i] = copies
    for i in range(3):
        wait_all(flying[i])
        total = m[i][pos[orders[i][1]]].astype(F32)
        for k in range(3):
            total += t[i][k].astype(F32)
        n[i][...] = total.astype(BF16)
        axis = orders[i][2]
        copies = []
        for step in range(1, 4):
            to = moved(pos, axis, step)
            copies.append(
                remote(n[i].at[to[axis]], v[i].at[step - 1], sums, 120 + i * 8 + 4 + step, device_of(to, core))
            )
        for copy in copies:
            copy.start()
        flying[i] = copies

    kk, ll, cp = (k0, k1, k2), (l0, l1, l2), (c0, c1, c2)
    for i in range(3):
        wait_all(flying[i])
        mine = pos[orders[i][2]]
        total = n[i][mine].astype(F32)
        for k in range(3):
            total += v[i][k].astype(F32)
        kk[i][mine] = (0.5 * (total * (1.0 / (BLOCK * LMAX)))).astype(BF16)
        axis = orders[i][2]
        copies = [
            remote(kk[i].at[mine], kk[i].at[mine], (g_send, g_recv), i * 16 + step, device_of(moved(pos, axis, step), core))
            for step in range(1, 4)
        ]
        for copy in copies:
            copy.start()
        flying[i] = copies
    for i in range(3):
        wait_all(flying[i])
        axis = orders[i][1]
        mine = pos[axis]
        copies = [pltpu.make_async_copy(kk[i], ll[i].at[mine], g_recv.at[i * 16 + 4])]
        for step in range(1, 4):
            copies.append(
                remote(kk[i], ll[i].at[mine], (g_send, g_recv), i * 16 + 4 + step, device_of(moved(pos, axis, step), core))
            )
        for copy in copies:
            copy.start()
        flying[i] = copies
    for i in range(3):
        wait_all(flying[i])
        axis = orders[i][0]
        mine = pos[axis]
        copies = [pltpu.make_async_copy(ll[i], cp[i].at[mine, core], g_recv.at[i * 16 + 8])]
        for step in range(1, 4):
            copies.append(
                remote(ll[i], cp[i].at[mine, core], (g_send, g_recv), i * 16 + 8 + step, device_of(moved(pos, axis, step), core))
            )
        for copy in copies:
            copy.start()
        flying[i] = copies
    passed = []
    for step in (0, 1, 3, 2):
        for i in range(3):
            axis = orders[i][0]
            flying[i][step].wait()
            at = lax.rem(pos[axis] + 4 - step, 4)
            copy = remote(cp[i].at[at, core], cp[i].at[at, core], (x_send, x_recv), i * 4 + step, device_of(pos, 1 - core))
            copy.start()
            passed.append(copy)
    wait_all(passed)

    s, back, turn, out = (s0, s1, s2), (h0, h1, h2), (i0, i1, i2), (f0_hbm, f1_hbm, f2_hbm)
    sems = (o_send, o_recv)

    def shift_part(i, carry):
        y = part_of(pos, i)

        def shift(j, inner):
            z, x, c = j >> 3, (j >> 1) & 3, j & 1
            g = z * 32 + x * 8 + c * 4 + y
            third = c2[y, c, z, x]
            third = jnp.concatenate([third[:, 0:64], third[:, 64:128]], axis=0)
            pair = jnp.concatenate([c0[z, c, x, y], c1[x, c, y, z]], axis=0)
            weights = jnp.concatenate([pair, third], axis=1)
            moved_by = jnp.dot(weights, partners(g), preferred_element_type=F32).astype(BF16)
            s0[z, c, x, y] = moved_by[0:48, 0:128]
            s1[x, c, y, z] = moved_by[0:48, 128:256]
            s2[y, c, z, x, 0:16] = moved_by[48:64, 0:128]
            s2[y, c, z, x, 16:32] = moved_by[48:64, 128:256]
            return inner

        lax.fori_loop(0, 32, shift, 0, unroll=2)
        start_part(pos, core, s, back, sems, i)
        return carry

    lax.fori_loop(0, 4, shift_part, 0)
    for i in range(3):
        wait_one(i, pos, core, s, back, sems)
        flying[i] = stage_two(i, pos, core, back[i], turn[i], sems)
    for i in range(3):
        wait_all(flying[i])
        flying[i] = stage_three(i, pos, core, turn[i], out[i], sems)
    for i in range(3):
        wait_all(flying[i])
    store.wait()


ROWS = (48, 48, 32)


def run_orthonormalize(
    functions, filter_taps, potential, energies, region_start, region_length, partner_groups
):
    anywhere = pl.BlockSpec(memory_space=pltpu.HBM)
    whole = pl.BlockSpec(memory_space=pltpu.VMEM)
    dma = pltpu.SemaphoreType.DMA

    def vmem(*shape, kind=BF16):
        return pltpu.VMEM(shape, kind)

    return pl.pallas_call(
        orthonormalize,
        out_shape=tuple(jax.ShapeDtypeStruct((4, 4, 4, 2, r, 128), BF16) for r in ROWS)
        + (jax.ShapeDtypeStruct((GROUP, NC), BF16), jax.ShapeDtypeStruct((GROUP, GROUP), BF16)),
        in_specs=[pl.BlockSpec(memory_space=pltpu.SMEM), anywhere] + [whole] * 5,
        out_specs=(anywhere,) * 4 + (whole,),
        scratch_shapes=[
            vmem(GROUP, NC),
            vmem(512, 512),
            vmem(4, 768, 256),
            vmem(2, 512, 256, kind=F32),
            vmem(GROUP, NC),
            vmem(128, 128, kind=F32),
            vmem(GROUP, 128, kind=F32),
            vmem(1, 128, kind=F32),
        ]
        + [vmem(4, 2, 4, 4, 32, 128)] * 6
        + [vmem(4, 4, 2, 4, 32, 128)] * 3
        + [vmem(4, 4, 4, 2, 32, 128)] * 3
        + [vmem(4, 2, 1, 128, kind=F32), vmem(4, 4, 2, 1, 128, kind=F32), vmem(4, 4, 4, 2, 1, 128, kind=F32)]
        + [vmem(GROUP, 128, kind=F32), vmem(128, GROUP, 128)]
        + [vmem(4, 2, 4, 4, 32, 128)] * 6
        + [vmem(4, 4, 32, 128)] * 3
        + [vmem(3, 4, 32, 128)] * 3
        + [vmem(4, 32, 128)] * 3
        + [vmem(3, 32, 128)] * 3
        + [vmem(4, 32, 128)] * 3
        + [vmem(4, 4, 32, 128)] * 3
        + [vmem(4, 2, 4, 4, 32, 128)] * 3
        + [vmem(4, 2, 4, 4, r, 128) for r in ROWS]
        + [vmem(4, 2, 4, 4, r, 128) for r in ROWS]
        + [vmem(4, 4, 2, 4, r, 128) for r in ROWS]
        + [dma, dma, dma((SEMS,)), dma((SEMS,)), dma((16,)), dma((16,)), dma((SEMS,)), dma((SEMS,))]
        + [dma((48,)), dma((48,)), dma((12,)), dma((12,)), dma((SEMS,)), dma((SEMS,))],
        compiler_params=pltpu.CompilerParams(
            collective_id=0, has_side_effects=True, vmem_limit_bytes=63 * 1024 * 1024
        ),
    )(
        partner_groups.T,
        functions,
        filter_taps.reshape(1, TAPS),
        energies.reshape(1, GROUP),
        region_start.reshape(1, GROUP),
        region_length.reshape(1, GROUP),
        potential.reshape(256, 128),
    )


def finish(own_ref, r_hbm, f0_hbm, f1_hbm, f2_hbm, o_hbm, r_ref, f0_ref, f1_ref, f2_ref, o_ref, in_sem, out_sem):
    weights = own_ref[...]
    low = lax.broadcasted_iota(jnp.int32, (GROUP, 128), 1) < 64

    def loads(i):
        z, x = lax.div(i, 2), lax.rem(i, 2) * 2
        pairs = []
        for k, (slab, count) in enumerate(((i, 1), (i + 24, 1), (8 + 2 * i, 2))):
            cut = pl.ds(pl.multiple_of(slab * 1024, 1024), count * 1024)
            pairs.append((r_hbm.at[:, cut], r_ref.at[:, cut]))
        cut = pl.ds(x, 2)
        pairs.append((f0_hbm.at[:, cut, z], f0_ref.at[:, cut, z]))
        pairs.append((f1_hbm.at[z, :, cut], f1_ref.at[z, :, cut]))
        pairs.append((f2_hbm.at[cut, z], f2_ref.at[cut, z]))
        return [pltpu.make_async_copy(a, b, in_sem.at[i, k]) for k, (a, b) in enumerate(pairs)]

    def stores(i):
        out = []
        for k, (slab, count) in enumerate(((i, 1), (i + 24, 1), (8 + 2 * i, 2))):
            cut = pl.ds(pl.multiple_of(slab * 1024, 1024), count * 1024)
            out.append(pltpu.make_async_copy(o_ref.at[:, cut], o_hbm.at[:, cut], out_sem.at[i, k]))
        return out

    def each(make):
        def body(i, carry):
            for copy in make(i):
                copy.start()
            return carry

        return body

    lax.fori_loop(0, 8, each(loads), 0)

    def slab_part(slab, y, h, moved_by):
        at = pl.ds(pl.multiple_of(slab * 1024 + y * 256 + h * 128, 128), 128)
        rows = r_ref[:, at]
        shifted = jnp.dot(weights, rows, preferred_element_type=F32)
        o_ref[:, at] = (rows.astype(F32) - shifted - moved_by).astype(BF16)

    def step(i, carry):
        for copy in loads(i):
            copy.wait()
        z, x0 = lax.div(i, 2), lax.rem(i, 2) * 2
        for dx in range(2):
            x = x0 + dx
            for y in range(4):
                twos = []
                for c in range(2):
                    tail = f2_ref[x, z, y, c].astype(F32)
                    single = jnp.concatenate([f0_ref[y, x, z, c].astype(F32), tail[0:16]], axis=0)
                    slab_part(8 + 2 * i + dx, y, c, single)
                    twos.append(jnp.concatenate([f1_ref[z, y, x, c].astype(F32), tail[16:32]], axis=0))
                slab_part(i, y, dx, jnp.where(low, twos[0], pltpu.roll(twos[1], 64, 1)))
                slab_part(i + 24, y, dx, jnp.where(low, pltpu.roll(twos[0], 64, 1), twos[1]))
        for copy in stores(i):
            copy.start()
        return carry

    lax.fori_loop(0, 8, step, 0)

    def last(i, carry):
        for copy in stores(i):
            copy.wait()
        return carry

    lax.fori_loop(0, 8, last, 0)


def run_finish(own, refined, f0, f1, f2):
    anywhere = pl.BlockSpec(memory_space=pltpu.HBM)
    return pl.pallas_call(
        finish,
        out_shape=jax.ShapeDtypeStruct((GROUP, NC), BF16),
        in_specs=[pl.BlockSpec(memory_space=pltpu.VMEM)] + [anywhere] * 4,
        out_specs=anywhere,
        scratch_shapes=[pltpu.VMEM((GROUP, NC), BF16)]
        + [pltpu.VMEM((4, 4, 4, 2, r, 128), BF16) for r in ROWS]
        + [pltpu.VMEM((GROUP, NC), BF16), pltpu.SemaphoreType.DMA((8, 6)), pltpu.SemaphoreType.DMA((8, 3))],
        compiler_params=pltpu.CompilerParams(vmem_limit_bytes=63 * 1024 * 1024),
    )(own, refined, f0, f1, f2)


def on_device(functions, filter_taps, potential, energies, region_start, region_length, partner_groups):
    f0, f1, f2, refined, own = run_orthonormalize(
        functions, filter_taps, potential, energies, region_start, region_length, partner_groups
    )
    return run_finish(own, refined, f0, f1, f2)


def solution(mesh):
    return jax.shard_map(
        on_device,
        mesh=mesh,
        in_specs=(
            P(("grid", "rep"), None),
            P(),
            P(),
            P(("grid", "rep")),
            P(("grid", "rep")),
            P(("grid", "rep")),
            P(),
        ),
        out_specs=P(("grid", "rep"), None),
        check_vma=False,
    )
```

time: 228 us -> 190 us (0.83)
  Pallas kernels: 213 us -> 190 us
  local copies, waits for them, and re-layouts: 11.1 us -> 0 us
  other arithmetic: 2.54 us -> 0 us
    pallas_call x1 -> x0, Pallas kernels: 62.9 us -> none  [run_exchange_in(): pl.pallas_call(exchange_in, out_shape=(piece, piece, piece, jax.ShapeDtyp...]
    pallas_call x1, Pallas kernels: 143 us -> 182 us  [run_orthonormalize(): pl.pallas_call(orthonormalize, out_shape=tuple((jax.ShapeDtypeStruct((4,...]
    unnamed x11 -> x0, local copies, waits for them, and re-layouts: 8.34 us -> none
where the time goes in v2:
time: 190 us
  Pallas kernels  190 us (100%)
    pallas_call x1, Pallas kernels, run_orthonormalize(): pl.pallas_call(orthonormalize, out_shape=tuple((jax.ShapeDtypeStruct((4,...  182 us
    pallas_call x1, Pallas kernels, run_finish(): pl.pallas_call(finish, out_shape=jax.ShapeDtypeStruct((GROUP, NC), BF16),...  7.1 us

profile of v2, /device:TPU:1, one launch (start us, length us, event | category | flops | bytes accessed | tf_op | source)
XLA Modules:
  0.0 189.6 jit_solution(4390404856823585778)
XLA Ops:
  0.0 182.5 %shard_map.73 = (bf16[4,4,4,2,48,128]{5,4,3,2,1,0:T(8,128)(2,1)}, bf16[4,4,4,2,48,128]{5,4,3,2,1,0:T(8,128)(2,1)}, bf16[4,4,4,2,32,128]{5,4,3,2,1,0:T(8,128)(2,1...) custom-call(s32[3,128]{1,0:T(4,128)} %bitcast.7, bf16[64,32768]{1,0:T(8,128)(2,1)} %fn_hbm.1, bf16[1,16]{1,0:T(2,128)(2,1)} %bitcast.8, ...), custom_call_target="tpu_custom_call" | custom-call | tf_op jit(solution)/shard_map/pallas_call | solution.py:596
  182.5 7.1 %shard_map.74 = bf16[64,32768]{1,0:T(8,128)(2,1)} custom-call(bf16[64,64]{1,0:T(8,128)(2,1)} %get-tuple-element.10.own_ref, bf16[64,32768]{1,0:T(8,128)(2,1)} %get-tuple-element.11.r_hbm, bf16[4,4,4,2,48,128]{5,4,3,2,1,0:T(8,128)(2,1)} %get-tuple-element.12.f0_hbm, bf16[4,4,4,2,48,128]{5,4,3,2,1,0:T(8,128)(2,1)} %get-tuple-element.13.f1_hbm, ...), custom_call_target="tpu_custom_call" | custom-call | tf_op jit(solution)/shard_map/pallas_call | solution.py:714

commit v3 on v2

--- a/solution.py
+++ b/solution.py
@@ -50,123 +50,86 @@
     pl.semaphore_wait(barrier, len(peers))
 
 
-def remote(src, dst, sems, index, device):
+def remote(src, dst, send_sem, recv_sem, device):
     return pltpu.make_async_remote_copy(
         src_ref=src,
         dst_ref=dst,
-        send_sem=sems[0].at[index],
-        recv_sem=sems[1].at[index],
+        send_sem=send_sem,
+        recv_sem=recv_sem,
         device_id=device,
         device_id_type=MESH,
     )
 
 
+def drain(ref, sem):
+    pltpu.make_async_copy(ref, ref, sem).wait()
+
+
 def part_of(pos, i):
     return lax.rem(pos[Y] + 1 + i, 4)
 
 
-def stage_one(t, pos, core, src, dst, sems, i):
+def start_one(t, pos, core, src, dst, sems, i):
     axis = ORDERS[t][0]
     mine = pos[axis]
     yy = part_of(pos, i)
-    remotes, local = [], None
+    send, recv = sems[0].at[0], sems[1].at[t]
     for step in (1, 3, 2, 0):
         for flip in (0, 1):
             c = core if flip == 0 else 1 - core
             to = moved(pos, axis, step)
-            index = t * 40 + i * 8 + step * 2 + flip
             if t == 0:
                 a, b = src.at[to[axis], c, :, yy], dst.at[mine, core, :, yy]
             else:
                 a, b = src.at[to[axis], c, yy], dst.at[mine, core, yy]
             if step == 0 and flip == 0:
-                local = pltpu.make_async_copy(a, b, sems[1].at[index])
+                local = pltpu.make_async_copy(a, b, recv)
             else:
-                remotes.append(remote(a, b, sems, index, device_of(to, c)))
-    return remotes + [local]
-
-
-def stage_one_y(pos, core, src, dst, sems, step, flips=(0, 1)):
+                remote(a, b, send, recv, device_of(to, c)).start()
+    local.start()
+
+
+def start_one_y(pos, core, src, dst, sems, step, flips=(0, 1)):
     mine = pos[Y]
     to = moved(pos, Y, step)
-    out = []
     for flip in flips:
         c = core if flip == 0 else 1 - core
-        out.append(
-            remote(src.at[to[Y], c], dst.at[mine, core], sems, 80 + step * 2 + flip, device_of(to, c))
-        )
-    return out
-
-
-def keep_y(pos, core, src, dst, sems):
-    return pltpu.make_async_copy(src.at[pos[Y], core], dst.at[pos[Y], core], sems[1].at[80])
+        remote(src.at[to[Y], c], dst.at[mine, core], sems[0].at[0], sems[1].at[2], device_of(to, c)).start()
 
 
 def start_part(pos, core, src, dst, sems, i):
     for t in (0, 1):
-        for copy in stage_one(t, pos, core, src[t], dst[t], sems, i):
-            copy.start()
+        start_one(t, pos, core, src[t], dst[t], sems, i)
 
     @pl.when(i < 3)
     def _():
-        for copy in stage_one_y(pos, core, src[2], dst[2], sems, i + 1):
-            copy.start()
+        start_one_y(pos, core, src[2], dst[2], sems, i + 1)
 
     @pl.when(i == 3)
     def _():
-        stage_one_y(pos, core, src[2], dst[2], sems, 0, (1,))[0].start()
-        keep_y(pos, core, src[2], dst[2], sems).start()
-
-
-def wait_one(t, pos, core, src, dst, sems):
-    if t < 2:
-        def body(i, carry):
-            wait_all(stage_one(t, pos, core, src[t], dst[t], sems, i))
-            return carry
-
-        lax.fori_loop(0, 4, body, 0)
-    else:
-        for step in range(1, 4):
-            wait_all(stage_one_y(pos, core, src[2], dst[2], sems, step))
-        stage_one_y(pos, core, src[2], dst[2], sems, 0, (1,))[0].wait()
-        keep_y(pos, core, src[2], dst[2], sems).wait()
-
-
-def stage_two(t, pos, core, src, dst, sems):
+        start_one_y(pos, core, src[2], dst[2], sems, 0, (1,))
+        pltpu.make_async_copy(
+            src[2].at[pos[Y], core], dst[2].at[pos[Y], core], sems[1].at[2]
+        ).start()
+
+
+def start_two(t, pos, core, src, dst, sems):
     axis = ORDERS[t][1]
     mine = pos[axis]
-    copies = []
-    for step in (1, 3, 2, 0):
+    send, recv = sems[0].at[1], sems[1].at[3 + t]
+    for step in (1, 3, 2):
         to = moved(pos, axis, step)
-        index = 120 + t * 8 + step
-        if step == 0:
-            copies.append(pltpu.make_async_copy(src.at[:, :, mine], dst.at[mine], sems[1].at[index]))
-        else:
-            copies.append(remote(src.at[:, :, to[axis]], dst.at[mine], sems, index, device_of(to, core)))
-    for copy in copies:
-        copy.start()
-    return copies
-
-
-def stage_three(t, pos, core, src, dst, sems):
+        remote(src.at[:, :, to[axis]], dst.at[mine], send, recv, device_of(to, core)).start()
+    pltpu.make_async_copy(src.at[:, :, mine], dst.at[mine], recv).start()
+
+
+def start_three(t, pos, core, src, dst, sems, recvs):
     axis = ORDERS[t][2]
     mine = pos[axis]
-    copies = []
-    for step in (1, 3, 2, 0):
+    for step in (1, 3, 2):
         to = moved(pos, axis, step)
-        index = 120 + t * 8 + 4 + step
-        if step == 0:
-            copies.append(pltpu.make_async_copy(src.at[:, :, :, mine], dst.at[mine], sems[1].at[index]))
-        else:
-            copies.append(
-                remote(src.at[:, :, :, to[axis]], dst.at[mine], sems, index, device_of(to, core))
-            )
-    for copy in copies:
-        copy.start()
-    return copies
-
-
-SEMS = 144
+        remote(src.at[:, :, :, to[axis]], dst.at[mine], sems[0].at[2], recvs[step], device_of(to, core)).start()
+    pltpu.make_async_copy(src.at[:, :, :, mine], dst.at[mine], recvs[0]).start()
 
 
 def wait_all(copies):
@@ -179,33 +142,48 @@
     return pos[order[0]], pos[order[1]], pos[order[2]]
 
 
-def tap_of(distance, taps_ref):
+def build_matrices(taps_ref, line_ref, plane_ref):
+    distance = (
+        lax.broadcasted_iota(jnp.int32, (SIDE, SIDE), 0)
+        - lax.broadcasted_iota(jnp.int32, (SIDE, SIDE), 1)
+        + TAPS // 2
+    )
     taps = taps_ref[...].astype(F32)
-    out = jnp.zeros(distance.shape, F32)
+    table = jnp.zeros((SIDE, SIDE), F32)
     for t in range(TAPS):
-        out = jnp.where(distance == t, jnp.broadcast_to(taps[:, t : t + 1], distance.shape), out)
-    return out
-
-
-def build_matrices(taps_ref, line_ref, plane_ref):
+        table = jnp.where(distance == t, jnp.broadcast_to(taps[:, t : t + 1], (SIDE, SIDE)), table)
+    table = table.astype(BF16)
+
+    def chosen(index):
+        lanes = lax.broadcasted_iota(jnp.int32, (256, SIDE), 1)
+        return jnp.where(index == lanes, 1.0, 0.0).astype(BF16)
+
+    def spread(a, b):
+        first = jnp.dot(a, table, preferred_element_type=F32).astype(BF16)
+        return lax.dot_general(first, b, (((1,), (1,)), ((), ())), preferred_element_type=F32)
+
+    place_of = lax.broadcasted_iota(jnp.int32, (256, SIDE), 0)
     rows = lax.broadcasted_iota(jnp.int32, (256, 256), 0)
     cols = lax.broadcasted_iota(jnp.int32, (256, 256), 1)
+    table_in = [chosen((place_of >> 4) + 16 * b) for b in range(2)]
     same = (rows & 15) == (cols & 15)
+    for b_out in range(2):
+        first = lax.dot_general(
+            table_in[b_out], table, (((1,), (1,)), ((), ())), preferred_element_type=F32
+        ).astype(BF16)
+        for b_in in range(2):
+            value = lax.dot_general(
+                first, table_in[b_in], (((1,), (1,)), ((), ())), preferred_element_type=F32
+            )
+            line_ref[b_out * 256 : b_out * 256 + 256, b_in * 256 : b_in * 256 + 256] = jnp.where(
+                same, value, 0.0
+            ).astype(BF16)
+    same = (rows & 31) == (cols & 31)
+    centre = chosen((place_of >> 5) + 8)
     for shift in (-1, 0, 1):
-        value = tap_of((cols >> 4) - (rows >> 4) + 16 * shift + TAPS // 2, taps_ref)
-        value = jnp.where(same, value, 0.0).astype(BF16)
+        value = jnp.where(same, spread(chosen((place_of >> 5) + 8 + 8 * shift), centre), 0.0)
         if shift == 0:
-            line_ref[0:256, 0:256] = value
-            line_ref[256:512, 256:512] = value
-        elif shift == 1:
-            line_ref[0:256, 256:512] = value
-        else:
-            line_ref[256:512, 0:256] = value
-    for shift in (-1, 0, 1):
-        value = tap_of((rows >> 5) - (cols >> 5) + 8 * shift + TAPS // 2, taps_ref)
-        value = jnp.where((rows & 31) == (cols & 31), value, 0.0)
-        if shift == 0:
-            inner = tap_of((rows & 31) - (cols & 31) + TAPS // 2, taps_ref)
+            inner = spread(chosen(place_of & 31), chosen(place_of & 31))
             value = value + jnp.where((rows >> 5) == (cols >> 5), inner, 0.0)
         value = value.astype(BF16)
         nothing = jnp.zeros_like(value)
@@ -316,7 +294,6 @@
 
     first_ref[...] = jnp.zeros((1, 128), F32)
     first_ref[0:1, 0:GROUP] = start_ref[...].astype(F32)
-    st_sems = (st_send, st_recv)
     starts = []
     for step in range(4):
         for flip in range(2):
@@ -324,9 +301,11 @@
             index = step * 2 + flip
             dst = st_a.at[pos[Z], core]
             if index == 0:
-                starts.append(pltpu.make_async_copy(first_ref, dst, st_recv.at[index]))
+                starts.append(pltpu.make_async_copy(first_ref, dst, st_recv.at[0]))
             else:
-                starts.append(remote(first_ref, dst, st_sems, index, device_of(moved(pos, Z, step), c)))
+                starts.append(
+                    remote(first_ref, dst, st_send.at[index], st_recv.at[0], device_of(moved(pos, Z, step), c))
+                )
 
     square_ref[...] = jnp.zeros((128, 128), F32)
     square_ref[0:1, 0:GROUP] = energy_ref[...]
@@ -351,29 +330,30 @@
     store = pltpu.make_async_copy(r_ref, r_hbm, store_sem)
     store.start()
 
-    wait_all(starts)
+    sent = starts[1:]
+    drain(st_a, st_recv.at[0])
     starts = []
     for step in range(4):
         dst = st_b.at[pos[X]]
         if step == 0:
-            starts.append(pltpu.make_async_copy(st_a, dst, st_recv.at[8 + step]))
+            starts.append(pltpu.make_async_copy(st_a, dst, st_recv.at[1]))
         else:
-            starts.append(remote(st_a, dst, st_sems, 8 + step, device_of(moved(pos, X, step), core)))
+            starts.append(remote(st_a, dst, st_send.at[8 + step], st_recv.at[1], device_of(moved(pos, X, step), core)))
     for copy in starts:
         copy.start()
 
-    flying = [None] * 3
     for t in range(3):
-        wait_one(t, pos, core, send, one, sems)
-        flying[t] = stage_two(t, pos, core, one[t], two[t], sems)
-    wait_all(starts)
+        drain(one[t], in_recv.at[t])
+        start_two(t, pos, core, one[t], two[t], sems)
+    sent += starts[1:]
+    drain(st_b, st_recv.at[1])
     starts = []
     for step in range(4):
         dst = st_c.at[pos[Y]]
         if step == 0:
-            starts.append(pltpu.make_async_copy(st_b, dst, st_recv.at[12 + step]))
+            starts.append(pltpu.make_async_copy(st_b, dst, st_recv.at[2]))
         else:
-            starts.append(remote(st_b, dst, st_sems, 12 + step, device_of(moved(pos, Y, step), core)))
+            starts.append(remote(st_b, dst, st_send.at[12 + step], st_recv.at[2], device_of(moved(pos, Y, step), core)))
     for copy in starts:
         copy.start()
 
@@ -391,10 +371,12 @@
     own_ref[...] = own.astype(BF16)
 
     for t in (2, 0, 1):
-        wait_all(flying[t])
-        flying[t] = stage_three(t, pos, core, two[t], got[t], sems)
-
-    wait_all(starts)
+        drain(two[t], in_recv.at[3 + t])
+        recvs = [in_recv.at[8 + step] if t == 2 else in_recv.at[6 + t] for step in range(4)]
+        start_three(t, pos, core, two[t], got[t], sems, recvs)
+
+    sent += starts[1:]
+    drain(st_c, st_recv.at[2])
     for i in range(128):
         y, x, z, c = i >> 5, (i >> 3) & 3, (i >> 1) & 3, i & 1
         square_ref[z * 32 + x * 8 + c * 4 + y : z * 32 + x * 8 + c * 4 + y + 1, :] = st_c[y, x, z, c]
@@ -404,10 +386,9 @@
 
     lower = lax.broadcasted_iota(jnp.int32, (GROUP, 128), 1) < 64
 
-    for k in (3, 0, 1, 2):
-        step = (1, 3, 2, 0)[k]
-        flying[2][k].wait()
+    for step in (0, 1, 3, 2):
         x = lax.rem(pos[X] + 4 - step, 4)
+        drain(g2.at[x], in_recv.at[8 + step])
 
         def unfold(j, carry, x=x):
             z, y, c = j >> 3, (j >> 1) & 3, j & 1
@@ -419,9 +400,9 @@
             u_ref[g] = jnp.where(keep, folded, 0.0).astype(BF16)
             return carry
 
-        lax.fori_loop(0, 32, unfold, 0, unroll=2)
-    wait_all(flying[0])
-    wait_all(flying[1])
+        lax.fori_loop(0, 32, unfold, 0, unroll=4)
+    drain(g0, in_recv.at[6])
+    drain(g1, in_recv.at[7])
 
     def columns(g):
         z, x, c, y = split(g)
@@ -452,7 +433,7 @@
             q2[y, c, z, x] = jnp.where(half_low, last[0:32], last[32:64]).astype(BF16)
             return inner
 
-        lax.fori_loop(0, 32, intersect, 0, unroll=2)
+        lax.fori_loop(0, 32, intersect, 0, unroll=4)
         start_part(pos, core, q, p, sums, i)
         return carry
 
@@ -460,89 +441,63 @@
 
     orders = ORDERS
     for i in range(3):
-        wait_one(i, pos, core, q, p, sums)
+        drain(p[i], r_recv.at[i])
         for j in range(4):
             total = p[i][0, 0, j].astype(F32)
             for k in range(1, 8):
                 total += p[i][k >> 1, k & 1, j].astype(F32)
             m[i][j] = total.astype(BF16)
         axis = orders[i][1]
-        copies = []
         for step in range(1, 4):
             to = moved(pos, axis, step)
-            copies.append(
-                remote(m[i].at[to[axis]], t[i].at[step - 1], sums, 120 + i * 8 + step, device_of(to, core))
-            )
-        for copy in copies:
-            copy.start()
-        flying[i] = copies
-    for i in range(3):
-        wait_all(flying[i])
+            remote(m[i].at[to[axis]], t[i].at[step - 1], r_send.at[1], r_recv.at[3 + i], device_of(to, core)).start()
+    for i in range(3):
+        drain(t[i], r_recv.at[3 + i])
         total = m[i][pos[orders[i][1]]].astype(F32)
         for k in range(3):
             total += t[i][k].astype(F32)
         n[i][...] = total.astype(BF16)
         axis = orders[i][2]
-        copies = []
         for step in range(1, 4):
             to = moved(pos, axis, step)
-            copies.append(
-                remote(n[i].at[to[axis]], v[i].at[step - 1], sums, 120 + i * 8 + 4 + step, device_of(to, core))
-            )
-        for copy in copies:
-            copy.start()
-        flying[i] = copies
+            remote(n[i].at[to[axis]], v[i].at[step - 1], r_send.at[2], r_recv.at[6 + i], device_of(to, core)).start()
 
     kk, ll, cp = (k0, k1, k2), (l0, l1, l2), (c0, c1, c2)
     for i in range(3):
-        wait_all(flying[i])
-        mine = pos[orders[i][2]]
+        drain(v[i], r_recv.at[6 + i])
+        axis = orders[i][2]
+        mine = pos[axis]
         total = n[i][mine].astype(F32)
         for k in range(3):
             total += v[i][k].astype(F32)
         kk[i][mine] = (0.5 * (total * (1.0 / (BLOCK * LMAX)))).astype(BF16)
-        axis = orders[i][2]
-        copies = [
-            remote(kk[i].at[mine], kk[i].at[mine], (g_send, g_recv), i * 16 + step, device_of(moved(pos, axis, step), core))
-            for step in range(1, 4)
-        ]
-        for copy in copies:
-            copy.start()
-        flying[i] = copies
-    for i in range(3):
-        wait_all(flying[i])
+        for step in range(1, 4):
+            to = device_of(moved(pos, axis, step), core)
+            remote(kk[i].at[mine], kk[i].at[mine], g_send.at[0], g_recv.at[i], to).start()
+    for i in range(3):
+        drain(v[i], g_recv.at[i])
         axis = orders[i][1]
         mine = pos[axis]
-        copies = [pltpu.make_async_copy(kk[i], ll[i].at[mine], g_recv.at[i * 16 + 4])]
+        pltpu.make_async_copy(kk[i], ll[i].at[mine], g_recv.at[3 + i]).start()
         for step in range(1, 4):
-            copies.append(
-                remote(kk[i], ll[i].at[mine], (g_send, g_recv), i * 16 + 4 + step, device_of(moved(pos, axis, step), core))
-            )
-        for copy in copies:
-            copy.start()
-        flying[i] = copies
-    for i in range(3):
-        wait_all(flying[i])
+            to = device_of(moved(pos, axis, step), core)
+            remote(kk[i], ll[i].at[mine], g_send.at[1], g_recv.at[3 + i], to).start()
+    for i in range(3):
+        drain(ll[i], g_recv.at[3 + i])
         axis = orders[i][0]
         mine = pos[axis]
-        copies = [pltpu.make_async_copy(ll[i], cp[i].at[mine, core], g_recv.at[i * 16 + 8])]
+        pltpu.make_async_copy(ll[i], cp[i].at[mine, core], g_recv.at[6 + i * 4]).start()
         for step in range(1, 4):
-            copies.append(
-                remote(ll[i], cp[i].at[mine, core], (g_send, g_recv), i * 16 + 8 + step, device_of(moved(pos, axis, step), core))
-            )
-        for copy in copies:
-            copy.start()
-        flying[i] = copies
-    passed = []
+            to = device_of(moved(pos, axis, step), core)
+            remote(ll[i], cp[i].at[mine, core], g_send.at[2], g_recv.at[6 + i * 4 + step], to).start()
     for step in (0, 1, 3, 2):
         for i in range(3):
-            axis = orders[i][0]
-            flying[i][step].wait()
-            at = lax.rem(pos[axis] + 4 - step, 4)
-            copy = remote(cp[i].at[at, core], cp[i].at[at, core], (x_send, x_recv), i * 4 + step, device_of(pos, 1 - core))
-            copy.start()
-            passed.append(copy)
-    wait_all(passed)
+            at = lax.rem(pos[orders[i][0]] + 4 - step, 4)
+            here = cp[i].at[at, core]
+            drain(here, g_recv.at[6 + i * 4 + step])
+            remote(here, here, x_send, x_recv.at[i], device_of(pos, 1 - core)).start()
+    for i in range(3):
+        drain(cp[i].at[:, 1 - core], x_recv.at[i])
 
     s, back, turn, out = (s0, s1, s2), (h0, h1, h2), (i0, i1, i2), (f0_hbm, f1_hbm, f2_hbm)
     sems = (o_send, o_recv)
@@ -564,20 +519,41 @@
             s2[y, c, z, x, 16:32] = moved_by[48:64, 128:256]
             return inner
 
-        lax.fori_loop(0, 32, shift, 0, unroll=2)
+        lax.fori_loop(0, 32, shift, 0, unroll=4)
         start_part(pos, core, s, back, sems, i)
         return carry
 
     lax.fori_loop(0, 4, shift_part, 0)
     for i in range(3):
-        wait_one(i, pos, core, s, back, sems)
-        flying[i] = stage_two(i, pos, core, back[i], turn[i], sems)
-    for i in range(3):
-        wait_all(flying[i])
-        flying[i] = stage_three(i, pos, core, turn[i], out[i], sems)
-    for i in range(3):
-        wait_all(flying[i])
+        drain(back[i], o_recv.at[i])
+        start_two(i, pos, core, back[i], turn[i], sems)
+    for i in range(3):
+        drain(turn[i], o_recv.at[3 + i])
+        start_three(i, pos, core, turn[i], out[i], sems, [o_recv.at[6 + i]] * 4)
+
+    def sent_all(sem, pieces):
+        drain(fn_ref.at[:, 0 : pieces * 64], sem)
+
     store.wait()
+    for copy in sent:
+        copy.wait_send()
+    for sem_set in (in_send, r_send):
+        sent_all(sem_set.at[0], 3 * 7 * 16)
+    for stage in (1, 2):
+        sent_all(in_send.at[stage], 3 * 3 * 32)
+    few = e0.at[0:3, 0, 0:3]
+    one_each = e0.at[0:3, 0, 0:3, 0]
+    drain(few, r_send.at[1])
+    drain(one_each, r_send.at[2])
+    drain(one_each, g_send.at[0])
+    drain(few, g_send.at[1])
+    sent_all(g_send.at[2], 3 * 3 * 16)
+    sent_all(x_send, 3 * 4 * 16)
+    sent_all(o_send.at[0], 4 * 7 * 16)
+    sent_all(o_send.at[1], 4 * 3 * 32)
+    sent_all(o_send.at[2], 4 * 3 * 32)
+    for i in range(3):
+        drain(out[i], o_recv.at[6 + i])
 
 
 ROWS = (48, 48, 32)
@@ -625,8 +601,8 @@
         + [vmem(4, 2, 4, 4, r, 128) for r in ROWS]
         + [vmem(4, 2, 4, 4, r, 128) for r in ROWS]
         + [vmem(4, 4, 2, 4, r, 128) for r in ROWS]
-        + [dma, dma, dma((SEMS,)), dma((SEMS,)), dma((16,)), dma((16,)), dma((SEMS,)), dma((SEMS,))]
-        + [dma((48,)), dma((48,)), dma((12,)), dma((12,)), dma((SEMS,)), dma((SEMS,))],
+        + [dma, dma, dma((3,)), dma((12,)), dma((16,)), dma((3,)), dma((3,)), dma((9,))]
+        + [dma((3,)), dma((18,)), dma, dma((3,)), dma((3,)), dma((9,))],
         compiler_params=pltpu.CompilerParams(
             collective_id=0, has_side_effects=True, vmem_limit_bytes=63 * 1024 * 1024
         ),
@@ -655,13 +631,13 @@
         pairs.append((f0_hbm.at[:, cut, z], f0_ref.at[:, cut, z]))
         pairs.append((f1_hbm.at[z, :, cut], f1_ref.at[z, :, cut]))
         pairs.append((f2_hbm.at[cut, z], f2_ref.at[cut, z]))
-        return [pltpu.make_async_copy(a, b, in_sem.at[i, k]) for k, (a, b) in enumerate(pairs)]
+        return [pltpu.make_async_copy(a, b, in_sem.at[i]) for a, b in pairs]
 
     def stores(i):
         out = []
         for k, (slab, count) in enumerate(((i, 1), (i + 24, 1), (8 + 2 * i, 2))):
             cut = pl.ds(pl.multiple_of(slab * 1024, 1024), count * 1024)
-            out.append(pltpu.make_async_copy(o_ref.at[:, cut], o_hbm.at[:, cut], out_sem.at[i, k]))
+            out.append(pltpu.make_async_copy(o_ref.at[:, cut], o_hbm.at[:, cut], out_sem))
         return out
 
     def each(make):
@@ -674,39 +650,38 @@
 
     lax.fori_loop(0, 8, each(loads), 0)
 
-    def slab_part(slab, y, h, moved_by):
-        at = pl.ds(pl.multiple_of(slab * 1024 + y * 256 + h * 128, 128), 128)
+    def slab_part(slab, y, moved_by):
+        at = pl.ds(pl.multiple_of(slab * 1024 + y * 256, 256), 256)
         rows = r_ref[:, at]
         shifted = jnp.dot(weights, rows, preferred_element_type=F32)
+        moved_by = jnp.concatenate(moved_by, axis=1)
         o_ref[:, at] = (rows.astype(F32) - shifted - moved_by).astype(BF16)
 
     def step(i, carry):
-        for copy in loads(i):
-            copy.wait()
+        drain(r_ref.at[:, 0:8192], in_sem.at[i])
         z, x0 = lax.div(i, 2), lax.rem(i, 2) * 2
-        for dx in range(2):
-            x = x0 + dx
-            for y in range(4):
-                twos = []
+        for y in range(4):
+            lows, highs = [], []
+            for dx in range(2):
+                x = x0 + dx
+                ones, twos = [], []
                 for c in range(2):
                     tail = f2_ref[x, z, y, c].astype(F32)
-                    single = jnp.concatenate([f0_ref[y, x, z, c].astype(F32), tail[0:16]], axis=0)
-                    slab_part(8 + 2 * i + dx, y, c, single)
+                    ones.append(jnp.concatenate([f0_ref[y, x, z, c].astype(F32), tail[0:16]], axis=0))
                     twos.append(jnp.concatenate([f1_ref[z, y, x, c].astype(F32), tail[16:32]], axis=0))
-                slab_part(i, y, dx, jnp.where(low, twos[0], pltpu.roll(twos[1], 64, 1)))
-                slab_part(i + 24, y, dx, jnp.where(low, pltpu.roll(twos[0], 64, 1), twos[1]))
+                slab_part(8 + 2 * i + dx, y, ones)
+                turned = [pltpu.roll(two, 64, 1) for two in twos]
+                lows.append(jnp.where(low, twos[0], turned[1]))
+                highs.append(jnp.where(low, turned[0], twos[1]))
+            slab_part(i, y, lows)
+            slab_part(i + 24, y, highs)
         for copy in stores(i):
             copy.start()
         return carry
 
     lax.fori_loop(0, 8, step, 0)
 
-    def last(i, carry):
-        for copy in stores(i):
-            copy.wait()
-        return carry
-
-    lax.fori_loop(0, 8, last, 0)
+    drain(o_ref, out_sem)
 
 
 def run_finish(own, refined, f0, f1, f2):
@@ -718,7 +693,7 @@
         out_specs=anywhere,
         scratch_shapes=[pltpu.VMEM((GROUP, NC), BF16)]
         + [pltpu.VMEM((4, 4, 4, 2, r, 128), BF16) for r in ROWS]
-        + [pltpu.VMEM((GROUP, NC), BF16), pltpu.SemaphoreType.DMA((8, 6)), pltpu.SemaphoreType.DMA((8, 3))],
+        + [pltpu.VMEM((GROUP, NC), BF16), pltpu.SemaphoreType.DMA((8,)), pltpu.SemaphoreType.DMA],
         compiler_params=pltpu.CompilerParams(vmem_limit_bytes=63 * 1024 * 1024),
     )(own, refined, f0, f1, f2)
 

time: 190 us -> 165 us (0.87)
  Pallas kernels: 190 us -> 164 us
    pallas_call x1, Pallas kernels: 182 us -> 158 us  [run_orthonormalize(): pl.pallas_call(orthonormalize, out_shape=tuple((jax.ShapeDtypeStruct((4,...]
where the time goes in v3:
time: 165 us; the launch traced here: 164 us
  Pallas kernels  164 us (99%)
    pallas_call x1, Pallas kernels, run_orthonormalize(): pl.pallas_call(orthonormalize, out_shape=tuple((jax.ShapeDtypeStruct((4,...  158 us
    pallas_call x1, Pallas kernels, run_finish(): pl.pallas_call(finish, out_shape=jax.ShapeDtypeStruct((GROUP, NC), BF16),...  6.33 us

profile of v3, /device:TPU:1, one launch (start us, length us, event | category | flops | bytes accessed | tf_op | source)
XLA Modules:
  0.0 164.5 jit_solution(420095375055838143)
XLA Ops:
  0.0 158.1 %shard_map.73 = (bf16[4,4,4,2,48,128]{5,4,3,2,1,0:T(8,128)(2,1)}, bf16[4,4,4,2,48,128]{5,4,3,2,1,0:T(8,128)(2,1)}, bf16[4,4,4,2,32,128]{5,4,3,2,1,0:T(8,128)(2,1...) custom-call(s32[3,128]{1,0:T(4,128)} %bitcast.7, bf16[64,32768]{1,0:T(8,128)(2,1)} %fn_hbm.1, bf16[1,16]{1,0:T(2,128)(2,1)} %bitcast.8, ...), custom_call_target="tpu_custom_call" | custom-call | tf_op jit(solution)/shard_map/pallas_call | solution.py:572
  158.2 6.3 %shard_map.74 = bf16[64,32768]{1,0:T(8,128)(2,1)} custom-call(bf16[64,64]{1,0:T(8,128)(2,1)} %get-tuple-element.10.own_ref, bf16[64,32768]{1,0:T(8,128)(2,1)} %get-tuple-element.11.r_hbm, bf16[4,4,4,2,48,128]{5,4,3,2,1,0:T(8,128)(2,1)} %get-tuple-element.12.f0_hbm, bf16[4,4,4,2,48,128]{5,4,3,2,1,0:T(8,128)(2,1)} %get-tuple-element.13.f1_hbm, ...), custom_call_target="tpu_custom_call" | custom-call | tf_op jit(solution)/shard_map/pallas_call | solution.py:689
